TPU v7x, 32 devices: a whole 2x2x4 slice. The times are simulated.
32 devices in a mesh: fsdp: 4 (over z), replica: 2 (over x), tensor: 4 (over y, core).
Axes of the slice: x: 2, y: 2, z: 4, core: 2. Of those that a mesh axis runs over, the one named last changes fastest.
Arguments:
- tokens: bfloat16 [1024, 8192], P(('fsdp', 'replica')), may hold values from -6 to 6
- weight_codes: bfloat16 [8192, 14336], P('fsdp', 'tensor'), may hold values from -127 to 127, as said below
- scales: float32 [64, 14336], P('fsdp', 'tensor'), may hold values from 3e-05 to 0.0003
- cotangent: bfloat16 [1024, 14336], P(('fsdp', 'replica'), 'tensor'), may hold values from -6 to 6
- sign_bits: int32 [14336], P('tensor'), may hold values from 0 to 1
Outputs:
- activation: bfloat16 [1024, 14336], P(('fsdp', 'replica'), 'tensor')
- input_grad: bfloat16 [1024, 8192], P(('fsdp', 'replica'), 'tensor')
- grad_codes: float32 [8192, 14336], P(('fsdp', 'replica'), 'tensor')
Inputs may be any that keep to these rules, and one draw needn't show every extreme that they name: `weight_codes`: integer values, held exactly.
All inputs are finite; a program needn't handle non-finite values.
Results may differ from a plain program's by a relative error of at most 0.015.
Values may be sent and summed in bfloat16 or wider, within the bound.
A program may use at most 128 MiB of HBM per device.

v0:
```python
import functools

import jax
import jax.numpy as jnp
from jax import lax
from jax.experimental import pallas as pl
from jax.experimental.pallas import tpu as pltpu
from jax.sharding import PartitionSpec as P

HB = 128


def hadamard_table(length):
    indices = jnp.arange(length, dtype=jnp.int32)
    intersection_bits = jnp.bitwise_and(indices[:, None], indices[None, :])
    parity = jnp.zeros((length, length), jnp.int32)
    for bit_pos in range(length.bit_length() - 1):
        parity = parity + jnp.bitwise_and(jnp.right_shift(intersection_bits, bit_pos), 1)
    return (1 - 2 * (parity % 2)).astype(jnp.bfloat16)


def grad_kernel(scaling, turned_ref, mine_ref, other_ref, sign_ref, table_ref, out_ref, rotated):
    half, width = mine_ref.shape
    for part, ref in enumerate((mine_ref, other_ref)):
        for block in range(width // HB):
            cols = slice(block * HB, (block + 1) * HB)
            signed = ref[:, cols] * sign_ref[:, cols]
            rotated[part * half:(part + 1) * half, cols] = jnp.dot(
                signed, table_ref[...], preferred_element_type=jnp.float32
            ).astype(jnp.bfloat16)
    out_ref[...] = scaling * jnp.dot(turned_ref[...], rotated[...], preferred_element_type=jnp.float32)


def rotated_grad(turned, mine, other, sign_bits):
    rows, total = turned.shape
    half, width = mine.shape
    tile = next(t for t in (512, 256, HB) if width % t == 0)
    signs = (2 * sign_bits - 1).astype(jnp.bfloat16)[None, :]
    scaling = float(1.0 / (HB * total) ** 0.5)
    column = lambda c: (0, c)
    fixed = lambda c: (0, 0)
    return pl.pallas_call(
        functools.partial(grad_kernel, scaling),
        grid=(width // tile,),
        out_shape=jax.ShapeDtypeStruct((rows, width), jnp.float32),
        in_specs=[
            pl.BlockSpec((rows, total), fixed),
            pl.BlockSpec((half, tile), column),
            pl.BlockSpec((half, tile), column),
            pl.BlockSpec((1, tile), column),
            pl.BlockSpec((HB, HB), fixed),
        ],
        out_specs=pl.BlockSpec((rows, tile), column),
        scratch_shapes=[pltpu.VMEM((total, tile), jnp.bfloat16)],
        compiler_params=pltpu.CompilerParams(vmem_limit_bytes=48 * 1024 * 1024),
        cost_estimate=pl.CostEstimate(
            flops=2 * rows * total * width, bytes_accessed=4 * rows * width + 2 * total * width, transcendentals=0
        ),
        name="rotated_grad",
    )(turned, mine, other, signs, hadamard_table(HB))


MESH = pl.DeviceIdType.MESH


def fetch_kernel(
    n, tokens_ref, codes_ref, scales_ref, weight_ref, columns_ref, came,
    out_sent, out_came, mate_sent, mate_came, over_sent, over_came, relay_sent, relay_came,
):
    step, last = pl.program_id(0), pl.num_programs(0) - 1
    me, t = lax.axis_index("fsdp"), lax.axis_index("tensor")
    mate, over = t + 1 - 2 * (t % 2), (t + 2) % 4
    rows = tokens_ref.shape[0]
    depth = tokens_ref.shape[1] // n
    piece = depth // 4

    def spot(s, q):
        return came.at[
            pl.ds(pl.multiple_of(s * rows, rows), rows), pl.ds(pl.multiple_of(q * piece, piece), piece)
        ]

    def send_out(f):
        start = pl.multiple_of(f * depth + t * piece, piece)
        return pltpu.make_async_remote_copy(
            src_ref=tokens_ref.at[:, pl.ds(start, piece)], dst_ref=spot(me, t),
            send_sem=out_sent.at[f], recv_sem=out_came.at[me],
            device_id={"fsdp": f}, device_id_type=MESH,
        )

    def receive_out(s):
        return pltpu.make_async_remote_copy(
            src_ref=spot(s, t), dst_ref=spot(s, t),
            send_sem=out_sent.at[s], recv_sem=out_came.at[s],
            device_id={"fsdp": s}, device_id_type=MESH,
        )

    def pass_on(s, q, sent, arrival, device):
        return pltpu.make_async_remote_copy(
            src_ref=spot(s, q), dst_ref=spot(s, q), send_sem=sent.at[s], recv_sem=arrival.at[s],
            device_id={"tensor": device}, device_id_type=MESH,
        )

    def to_mate(s):
        return pass_on(s, t, mate_sent, mate_came, mate)

    def to_over(s):
        return pass_on(s, t, over_sent, over_came, over)

    def to_relay(s):
        return pass_on(s, over, relay_sent, relay_came, mate)

    @pl.when(step == 0)
    def _():
        barrier = pltpu.get_barrier_semaphore()
        for k in range(1, n):
            pl.semaphore_signal(barrier, inc=1, device_id={"fsdp": (me + k) % n}, device_id_type=MESH)
        pl.semaphore_signal(barrier, inc=1, device_id={"tensor": mate}, device_id_type=MESH)
        pl.semaphore_signal(barrier, inc=1, device_id={"tensor": over}, device_id_type=MESH)
        pl.semaphore_wait(barrier, n + 1)
        for k in range(1, n):
            send_out((me + k) % n).start()
        came[pl.ds(pl.multiple_of(me * rows, rows), rows), :] = tokens_ref[
            :, pl.ds(pl.multiple_of(me * depth, depth), depth)
        ]

    weight_ref[...] = (
        codes_ref[...].astype(jnp.float32) * scales_ref[pl.ds(step, 1), :]
    ).astype(jnp.bfloat16)

    def each(k, act):
        for s in (me - k, me + k):
            @pl.when(jnp.logical_and(s >= 0, s < n))
            def _():
                act(s)

    def forward(s):
        receive_out(s).wait_recv()
        to_mate(s).start()
        to_over(s).start()

    def relay(s):
        to_over(s).wait_recv()
        to_relay(s).start()

    for k in range(1, n):
        @pl.when(step == jnp.minimum(2 + 3 * k, last))
        def _():
            each(k, forward)

    for k in range(1, n):
        @pl.when(step == jnp.minimum(5 + 3 * k, last))
        def _():
            each(k, relay)

    def finish(s):
        to_mate(s).wait_recv()
        to_relay(s).wait_recv()
        send_out(s).wait_send()
        to_mate(s).wait_send()
        to_over(s).wait_send()
        to_relay(s).wait_send()

    @pl.when(step == last)
    def _():
        for k in range(1, n):
            each(k, finish)
        columns_ref[...] = came[...]


def fetch_tokens(tokens, codes, scales, n):
    rows, width = tokens.shape
    shard_rows, cols = codes.shape
    steps = scales.shape[0]
    fixed = lambda i: (0, 0)
    sem = pltpu.SemaphoreType.DMA((n,))
    return pl.pallas_call(
        functools.partial(fetch_kernel, n),
        grid=(steps,),
        out_shape=(
            jax.ShapeDtypeStruct(codes.shape, jnp.bfloat16),
            jax.ShapeDtypeStruct((n * rows, shard_rows), jnp.bfloat16),
        ),
        in_specs=[
            pl.BlockSpec((rows, width), fixed),
            pl.BlockSpec((shard_rows // steps, cols), lambda i: (i, 0)),
            pl.BlockSpec((steps, cols), fixed),
        ],
        out_specs=(
            pl.BlockSpec((shard_rows // steps, cols), lambda i: (i, 0)),
            pl.BlockSpec((n * rows, shard_rows), fixed),
        ),
        scratch_shapes=[pltpu.VMEM((n * rows, shard_rows), jnp.bfloat16)] + [sem] * 8,
        compiler_params=pltpu.CompilerParams(
            collective_id=1, has_side_effects=True, vmem_limit_bytes=48 * 1024 * 1024
        ),
        name="fetch_tokens",
    )(tokens, codes, scales)


def line_kernel(
    n, width, tokens_ref, weight_hbm, cot_ref, act_ref, mine_ref, other_ref, product_ref, across_ref,
    part_ref, sums, from_left, from_right, total, weight_ref, gathered, fetched, swap_sent, swap_came, pair_sent, pair_came,
    sum_sent, left_came, right_came, up_sent, down_sent, came, cross_sent, cross_came,
):
    me = lax.axis_index("fsdp")
    partner_id = 1 - lax.axis_index("replica")
    mate = lax.axis_index("tensor") + 1 - 2 * (lax.axis_index("tensor") % 2)
    high = jnp.minimum(me + 1, n - 1)
    low = jnp.maximum(me - 1, 0)
    rows = cot_ref.shape[0]
    blocks = cot_ref.shape[1] // width
    has_low, has_high = me > 0, me < n - 1

    def at(ref, owner, c):
        start = owner * rows if isinstance(owner, int) else pl.multiple_of(owner * rows, rows)
        return ref.at[pl.ds(start, rows), pl.ds(pl.multiple_of(c * width, width), width)]

    def move(source, target, owner, c, send, recv, device):
        return pltpu.make_async_remote_copy(
            src_ref=at(source, owner, c), dst_ref=at(target, owner, c),
            send_sem=send.at[owner, c], recv_sem=recv.at[owner, c],
            device_id=device, device_id_type=MESH,
        )

    def sum_up(d, c):
        return move(sums, from_left, d, c, sum_sent, left_came, {"fsdp": high})

    def sum_down(d, c):
        return move(sums, from_right, d, c, sum_sent, right_came, {"fsdp": low})

    def go_up(s, c):
        return move(mine_ref, mine_ref, s, c, up_sent, came, {"fsdp": high})

    def go_down(s, c):
        return move(mine_ref, mine_ref, s, c, down_sent, came, {"fsdp": low})

    def cross(s, c):
        return move(mine_ref, other_ref, s, c, cross_sent, cross_came, {"replica": partner_id})

    def within(c):
        return jnp.logical_and(c >= 0, c < blocks)

    def fetch(c):
        cols = pl.ds(pl.multiple_of(c * width, width), width)
        return pltpu.make_async_copy(weight_hbm.at[:, cols], weight_ref.at[:, cols], fetched.at[c])

    def fetch_all(c, carry):
        fetch(c).start()
        return carry

    lax.fori_loop(0, blocks, fetch_all, 0)

    def project(c):
        fetch(c).wait()
        cols = pl.ds(pl.multiple_of(c * width, width), width)
        part_ref[:, cols] = jnp.dot(
            tokens_ref[...], weight_ref[:, cols], preferred_element_type=jnp.float32
        ).astype(jnp.bfloat16)

    barrier = pltpu.get_barrier_semaphore()
    pl.semaphore_signal(barrier, inc=1, device_id={"replica": partner_id}, device_id_type=MESH)
    pl.semaphore_signal(barrier, inc=1, device_id={"tensor": mate}, device_id_type=MESH)

    @pl.when(has_low)
    def _():
        pl.semaphore_signal(barrier, inc=1, device_id={"fsdp": low}, device_id_type=MESH)

    @pl.when(has_high)
    def _():
        pl.semaphore_signal(barrier, inc=1, device_id={"fsdp": high}, device_id_type=MESH)

    pl.semaphore_wait(barrier, 2 + jnp.where(has_low, 1, 0) + jnp.where(has_high, 1, 0))

    depth = across_ref.shape[1]
    small = depth // 2
    lane = lax.axis_index("tensor") % 2
    share = across_ref.at[:, pl.ds(pl.multiple_of(lane * small, small), small)]
    start = pl.multiple_of(partner_id * depth + lane * small, small)
    swap = pltpu.make_async_remote_copy(
        src_ref=tokens_ref.at[:, pl.ds(start, small)],
        dst_ref=share, send_sem=swap_sent, recv_sem=swap_came,
        device_id={"replica": partner_id}, device_id_type=MESH,
    )
    pair = pltpu.make_async_remote_copy(
        src_ref=share, dst_ref=share, send_sem=pair_sent, recv_sem=pair_came,
        device_id={"tensor": mate}, device_id_type=MESH,
    )
    swap.start()
    gathered[...] = jnp.zeros_like(gathered)
    project(0)

    def reduce_chain(c, first, owners, applies, arrival, send):
        @pl.when(within(c))
        def _():
            for d in owners:
                @pl.when(applies(d))
                def _():
                    @pl.when(first)
                    def _():
                        at(sums, d, c)[...] = at(part_ref, d, c)[...]

                    @pl.when(jnp.logical_not(first))
                    def _():
                        arrival[1](d, c).wait_recv()
                        at(sums, d, c)[...] = (
                            at(part_ref, d, c)[...].astype(jnp.float32)
                            + at(arrival[0], d, c)[...].astype(jnp.float32)
                        ).astype(jnp.bfloat16)
            for d in owners:
                @pl.when(applies(d))
                def _():
                    send(d, c).start()

    def step(i, carry):
        reduce_chain(
            i - me, me == 0, range(n - 1, 0, -1), lambda d: me < d, (from_left, sum_up), sum_up
        )
        reduce_chain(
            i - (n - 1 - me), me == n - 1, range(n - 1), lambda d: me > d, (from_right, sum_down), sum_down
        )
        c = i - (n - 1)

        @pl.when(within(c))
        def _():
            total[...] = at(part_ref, me, c)[...].astype(jnp.float32)

            @pl.when(has_low)
            def _():
                sum_up(me, c).wait_recv()
                total[...] += at(from_left, me, c)[...].astype(jnp.float32)

            @pl.when(has_high)
            def _():
                sum_down(me, c).wait_recv()
                total[...] += at(from_right, me, c)[...].astype(jnp.float32)

            hidden = total[...]
            sig = jax.nn.sigmoid(hidden)
            at(act_ref, 0, c)[...] = (hidden * sig).astype(jnp.bfloat16)
            at(mine_ref, me, c)[...] = (
                at(cot_ref, 0, c)[...].astype(jnp.float32) * sig * (1.0 + hidden * (1.0 - sig))
            ).astype(jnp.bfloat16)

            @pl.when(has_high)
            def _():
                go_up(me, c).start()

            @pl.when(has_low)
            def _():
                go_down(me, c).start()

            cross(me, c).start()

        for k in range(1, n):
            late = i - (n - 1 + k)

            @pl.when(jnp.logical_and(within(late), me - k >= 0))
            def _():
                s = me - k
                go_up(s, late).wait_recv()

                @pl.when(has_high)
                def _():
                    go_up(s, late).start()

                cross(s, late).start()

            @pl.when(jnp.logical_and(within(late), me + k < n))
            def _():
                s = me + k
                go_down(s, late).wait_recv()

                @pl.when(has_low)
                def _():
                    go_down(s, late).start()

                cross(s, late).start()

        @pl.when(i == blocks - 1)
        def _():
            swap.wait()
            pair.start()

        @pl.when(i + 1 < blocks)
        def _():
            project(i + 1)

        done = i - 2 * (n - 1)

        @pl.when(done >= 0)
        def _():
            cols = pl.ds(pl.multiple_of(done * width, width), width)
            gathered[...] += lax.dot_general(
                mine_ref[:, cols], weight_ref[:, cols], (((1,), (1,)), ((), ())),
                preferred_element_type=jnp.float32,
            )

        return carry

    lax.fori_loop(0, blocks + 2 * (n - 1), step, 0)

    product_ref[...] = gathered[...].astype(jnp.bfloat16)
    pair.wait()

    def drain(c, carry):
        for d in range(n):
            @pl.when(me != d)
            def _():
                sum_up(d, c).wait_send()

            @pl.when(jnp.logical_and(has_high, me >= d))
            def _():
                go_up(d, c).wait_send()

            @pl.when(jnp.logical_and(has_low, me <= d))
            def _():
                go_down(d, c).wait_send()

            cross(d, c).wait_send()
            cross(d, c).wait_recv()
        return carry

    lax.fori_loop(0, blocks, drain, 0)


def line_exchange(columns, weight, cotangent, n):
    rows, depth = columns.shape
    cols = weight.shape[1]
    width = next(t for t in (256, HB) if cols % t == 0)
    vmem = pl.BlockSpec(memory_space=pltpu.VMEM)
    whole = jax.ShapeDtypeStruct((rows, cols), jnp.bfloat16)
    sems = pltpu.SemaphoreType.DMA((n, cols // width))
    return pl.pallas_call(
        functools.partial(line_kernel, n, width),
        out_shape=(
            jax.ShapeDtypeStruct(cotangent.shape, jnp.bfloat16),
            whole,
            whole,
            jax.ShapeDtypeStruct((rows, depth), jnp.bfloat16),
            jax.ShapeDtypeStruct((rows, depth // 2), jnp.bfloat16),
        ),
        in_specs=[vmem, pl.BlockSpec(memory_space=pl.ANY), vmem],
        out_specs=(vmem,) * 5,
        scratch_shapes=[pltpu.VMEM((rows, cols), jnp.bfloat16)] * 4
        + [
            pltpu.VMEM((rows // n, width), jnp.float32),
            pltpu.VMEM(weight.shape, jnp.bfloat16),
            pltpu.VMEM((rows, depth), jnp.float32),
            pltpu.SemaphoreType.DMA((cols // width,)),
            pltpu.SemaphoreType.DMA,
            pltpu.SemaphoreType.DMA,
            pltpu.SemaphoreType.DMA,
            pltpu.SemaphoreType.DMA,
        ]
        + [sems] * 8,
        compiler_params=pltpu.CompilerParams(
            collective_id=0, has_side_effects=True, vmem_limit_bytes=60 * 1024 * 1024
        ),
        name="line_exchange",
    )(columns, weight, cotangent)


def halve(array, keep, n_tensor, bit):
    lead = lax.dynamic_index_in_dim(array, keep, 0, keepdims=False)
    sent = lax.dynamic_index_in_dim(array, 1 - keep, 0, keepdims=False)
    came = lax.ppermute(sent, "tensor", [(t, t ^ bit) for t in range(n_tensor)])
    return (lead.astype(jnp.float32) + came.astype(jnp.float32)).astype(jnp.bfloat16)


def tensor_reduce(product, n_tensor):
    if n_tensor != 4:
        return lax.psum_scatter(product, "tensor", scatter_dimension=0, tiled=True)
    rows, cols = product.shape
    place = lax.axis_index("tensor")
    chunks = product.reshape(2, 2, rows // 4, cols).swapaxes(0, 1)
    chunks = halve(chunks, place % 2, n_tensor, 1)
    return halve(chunks, place // 2, n_tensor, 2)


def partner(array):
    return lax.ppermute(array, "replica", [(0, 1), (1, 0)])


def shards(tokens, weight_codes, scales, cotangent, sign_bits):
    n_fsdp, n_tensor = lax.axis_size("fsdp"), lax.axis_size("tensor")
    local_tokens = tokens.shape[0]
    shard_rows, hidden_cols = weight_codes.shape
    block_rows = shard_rows // scales.shape[0]
    if n_tensor == 4 and 1 < n_fsdp <= 4:
        weight, columns = fetch_tokens(tokens, weight_codes, scales, n_fsdp)
    else:
        weight = (
            (
                weight_codes.astype(jnp.float32).reshape(scales.shape[0], block_rows, hidden_cols)
                * scales[:, None, :]
            )
            .reshape(shard_rows, hidden_cols)
            .astype(jnp.bfloat16)
        )
        piece = shard_rows // n_tensor
        own = lax.dynamic_slice_in_dim(
            tokens.reshape(local_tokens, n_fsdp, shard_rows), lax.axis_index("tensor") * piece, piece, 2
        ).reshape(local_tokens, n_fsdp * piece)
        quarter = lax.all_to_all(own, "fsdp", split_axis=1, concat_axis=0, tiled=True)
        columns = lax.all_gather(quarter, "tensor", axis=1, tiled=True)
    half_rows = shard_rows // 2
    replica = lax.axis_index("replica")
    kept = lax.dynamic_slice_in_dim(columns, replica * half_rows, half_rows, 1)
    gathered = n_fsdp * local_tokens
    held = 2 * shard_rows * hidden_cols + 12 * gathered * hidden_cols + 9 * gathered * shard_rows
    if n_fsdp > 1 and n_tensor % 2 == 0 and held <= 52 * 1024 * 1024:
        activation, arrived, other, product, across = line_exchange(columns, weight, cotangent, n_fsdp)
    else:
        across = partner(lax.dynamic_slice_in_dim(columns, (1 - replica) * half_rows, half_rows, 1))
        hidden = lax.psum_scatter(
            jnp.dot(columns, weight, preferred_element_type=jnp.float32).astype(jnp.bfloat16),
            "fsdp",
            scatter_dimension=0,
            tiled=True,
        ).astype(jnp.float32)
        sigmoid_val = jax.nn.sigmoid(hidden)
        activation = (hidden * sigmoid_val).astype(jnp.bfloat16)
        hidden_grad = (
            cotangent.astype(jnp.float32) * sigmoid_val * (1.0 + hidden * (1.0 - sigmoid_val))
        ).astype(jnp.bfloat16)
        arrived = lax.all_gather(hidden_grad, "fsdp", axis=0, tiled=True)
        other = partner(arrived)
        product = lax.dot_general(
            arrived, weight, (((1,), (1,)), ((), ())), preferred_element_type=jnp.float32
        ).astype(jnp.bfloat16)
    turned = jnp.concatenate([kept, across], axis=0).T
    if n_fsdp == n_tensor:
        summed = tensor_reduce(product, n_tensor)
        swap = [(f * n_tensor + t, t * n_tensor + f) for f in range(n_fsdp) for t in range(n_tensor)]
        input_grad = lax.ppermute(summed, ("fsdp", "tensor"), swap)
    else:
        returned = lax.all_to_all(product, "fsdp", split_axis=0, concat_axis=1, tiled=True)
        input_grad = lax.psum_scatter(returned, "tensor", scatter_dimension=1, tiled=True)
    grad_codes = rotated_grad(turned, arrived, other, sign_bits)
    return (activation, input_grad, grad_codes)


def solution(mesh):
    return jax.shard_map(
        shards,
        mesh=mesh,
        in_specs=(
            P(("fsdp", "replica"), None),
            P("fsdp", "tensor"),
            P("fsdp", "tensor"),
            P(("fsdp", "replica"), "tensor"),
            P("tensor"),
        ),
        out_specs=(
            P(("fsdp", "replica"), "tensor"),
            P(("fsdp", "replica"), "tensor"),
            P(("fsdp", "replica"), "tensor"),
        ),
        check_vma=False,
    )
```

profile of v0, /device:TPU:4, one launch (start us, length us, event | category | flops | bytes accessed | tf_op | source)
XLA Modules:
  0.0 196.4 jit_solution(8767853878524928899)
XLA Ops:
  0.7 0.0 copy-start.2
  0.7 1.6 copy-done.2
  2.2 0.0 copy-start.3
  2.2 0.9 copy-done.3
  3.2 26.3 %fetch_tokens.1 = (bf16[2048,3584]{1,0:T(8,128)(2,1)}, bf16[512,2048]{1,0:T(8,128)(2,1)S(1)}) custom-call(bf16[128,8192]{1,0:T(8,128)(2,1)S(1)} %copy-done.2, bf16[2048,3584]{1,0:T(8,128)(2,1)} %codes_ref.1, f32[16,3584]{1,0:T(8,128)S(1)} %copy-done.3), custom_call_target="tpu_custom_call" | custom-call | tf_op jit(solution)/shard_map/fetch_tokens/pallas_call | solution.py:176
  29.5 0.0 copy-start
  29.5 1.3 copy-done
  30.8 112.7 %line_exchange.1 = (bf16[128,3584]{1,0:T(8,128)(2,1)}, bf16[512,3584]{1,0:T(8,128)(2,1)}, bf16[512,3584]{1,0:T(8,128)(2,1)}, bf16[512,2048]{1,0:T(8,128)(2,1)}, bf16[512,1024]{1,0:T(8,128)(2,1)}) custom-call(bf16[512,2048]{1,0:T(8,128)(2,1)} %copy-done, bf16[2048,3584]{1,0:T(8,128)(2,1)} %get-tuple-element.11.weight_hbm, bf16[128,3584]{1,0:T(8,128)(2,1)} %cot_ref.1), custom_call_target="tpu_custom_call" | custom-call | tf_op jit(solution)/shard_map/line_exchange/pallas_call | solution.py:433
  143.5 1.3 dynamic-slice_bitcast_fusion
  144.8 0.1 collective-permute-start
  144.9 0.0 copy-start.8
  145.0 0.0 copy-start.1
  145.0 2.7 %collective-permute-done = bf16[2,128,2048]{2,1,0:T(8,128)(2,1)} collective-permute-done((bf16[2,128,2048]{2,1,0:T(8,128)(2,1)S(1)}, bf16[2,128,2048]{2,1,0:T(8,128)(2,1)}, u32[]{:S(2)}, u32[]{:S(2)}) %collective-permute-start) | collective-permute-done | bytes 1048608 | tf_op jit(solution)/shard_map/ppermute | solution.py:466
  147.7 1.9 fusion
  149.6 0.8 dynamic-slice_bitcast_fusion.1
  150.5 1.0 collective-permute-start.1
  151.5 0.0 copy-done.8
  151.5 0.0 copy-done.1
  151.5 2.5 %copy.9 = bf16[512,2048]{0,1:T(8,128)(2,1)} copy(bf16[512,2048]{1,0:T(8,128)(2,1)S(1)} %copy-done.1) | data formatting | bytes 4194304 | tf_op jit(solution)/shard_map/fetch_tokens/pallas_call | solution.py:176
  154.0 0.0 copy-start.5
  154.0 2.4 %copy.10 = bf16[512,1024]{0,1:T(8,128)(2,1)} copy(bf16[512,1024]{1,0:T(8,128)(2,1)} %get-tuple-element.14) | data formatting | bytes 2097152 | tf_op jit(solution)/shard_map/line_exchange/pallas_call | solution.py:433
  156.5 0.0 copy-start.6
  156.5 0.1 fusion.5.table_ref
  156.6 0.0 copy-done.5
  156.6 0.1 constant_dynamic-slice_fusion
  156.7 1.0 copy-done.6
  157.7 0.0 copy-start.4
  157.7 0.3 maximum_bitcast_fusion.turned_ref
  158.0 6.7 %collective-permute-done.1 = bf16[128,2048]{1,0:T(8,128)(2,1)} collective-permute-done((bf16[128,2048]{1,0:T(8,128)(2,1)}, bf16[128,2048]{1,0:T(8,128)(2,1)}, u32[]{:S(2)}, u32[]{:S(2)}) %collective-permute-start.1) | collective-permute-done | bytes 524320 | tf_op jit(solution)/shard_map/ppermute | solution.py:466
  164.7 1.2 fusion.1
  165.9 3.0 %collective-permute-start.2 = (bf16[128,2048]{1,0:T(8,128)(2,1)S(1)}, bf16[128,2048]{1,0:T(8,128)(2,1)S(1)}, u32[]{:S(2)}, u32[]{:S(2)}) collective-permute-start(bf16[128,2048]{1,0:T(8,128)(2,1)S(1)} %fusion.1), channel_id=1, source_target_pairs={{0,0},{1,8},{2,16},{3,24},{8,1},{9,9},{10,17},{11,25},{16,2},{17,1... | collective-permute-start | bytes 1572872 | tf_op jit(solution)/shard_map/ppermute | solution.py:535
  168.9 0.0 copy-done.4
  168.9 0.0 copy-start.7
  168.9 13.3 %rotated_grad.1 = f32[1024,3584]{1,0:T(8,128)} custom-call(bf16[1024,1024]{1,0:T(8,128)(2,1)S(1)} %maximum_bitcast_fusion.turned_ref, bf16[512,3584]{1,0:T(8,128)(2,1)S(1)} %copy-done.4, bf16[512,3584]{1,0:T(8,128)(2,1)} %get-tuple-element.16.other_ref, bf16[1,3584]{1,0:T(2,128)(2,1)S(1)} %broadcast_in_dim.2.sign_ref, bf16[128,128]{1,0:T(8,128)(2,1)S(1)} %fusion.5.table_ref), custom_call_target="tpu_custom_call" | custom-call | flops 7516192768 | bytes 22020096 | tf_op jit(solution)/shard_map/rotated_grad/pallas_call | solution.py:42
  182.2 12.4 %collective-permute-done.2 = bf16[128,2048]{1,0:T(8,128)(2,1)S(1)} collective-permute-done((bf16[128,2048]{1,0:T(8,128)(2,1)S(1)}, bf16[128,2048]{1,0:T(8,128)(2,1)S(1)}, u32[]{:S(2)}, u32[]{:S(2)}) %collective-permute-start.2) | collective-permute-done | bytes 524320 | tf_op jit(solution)/shard_map/ppermute | solution.py:535
  194.7 0.0 copy-done.7
  194.7 0.9 copy.14
  195.6 0.8 copy.15
  (2 shorter events, 0.0 us)
Async XLA Ops:
  0.7 1.6 copy-start.2
  2.2 0.9 copy-start.3
  29.5 1.3 copy-start
  144.8 2.9 %collective-permute-start = (bf16[2,128,2048]{2,1,0:T(8,128)(2,1)S(1)}, bf16[2,128,2048]{2,1,0:T(8,128)(2,1)}, u32[]{:S(2)}, u32[]{:S(2)}) collective-permute-start(bf16[2,128,2048]{2,1,0:T(8,128)(2,1)S(1)} %dynamic-slice_bitcast_fusion), channel_id=1, source_target_pairs={{0,1},{1,0},{2,3},{3,2},{4,5},{5,4},{6,7},{7,6},{8,9},{9,8},{10,11... | collective-permute-start | bytes 3145736 | tf_op jit(solution)/shard_map/ppermute | solution.py:466
  144.9 6.6 %copy-start.8 = (s32[3584]{0:T(1024)S(1)}, s32[3584]{0:T(1024)}, u32[]{:S(2)}) copy-start(s32[3584]{0:T(1024)} %param.9) | copy-start | bytes 43012
  145.0 6.6 %copy-start.1 = (bf16[512,2048]{1,0:T(8,128)(2,1)S(1)}, bf16[512,2048]{1,0:T(8,128)(2,1)}, u32[]{:S(2)}) copy-start(bf16[512,2048]{1,0:T(8,128)(2,1)} %copy-done) | copy-start | bytes 6291460
  150.5 14.3 %collective-permute-start.1 = (bf16[128,2048]{1,0:T(8,128)(2,1)}, bf16[128,2048]{1,0:T(8,128)(2,1)}, u32[]{:S(2)}, u32[]{:S(2)}) collective-permute-start(bf16[128,2048]{1,0:T(8,128)(2,1)} %dynamic-slice_bitcast_fusion.1), channel_id=1, source_target_pairs={{0,2},{1,3},{2,0},{3,1},{4,6},{5,7},{6,4},{7,5},{8,10},{9,11},{10,... | collective-permute-start | bytes 1572872 | tf_op jit(solution)/shard_map/ppermute | solution.py:466
  154.0 2.6 %copy-start.5 = (bf16[512,2048]{0,1:T(8,128)(2,1)S(1)}, bf16[512,2048]{0,1:T(8,128)(2,1)}, u32[]{:S(2)}) copy-start(bf16[512,2048]{0,1:T(8,128)(2,1)} %copy.9) | copy-start | bytes 6291460
  156.5 1.2 copy-start.6
  157.7 11.2 %copy-start.4 = (bf16[512,3584]{1,0:T(8,128)(2,1)S(1)}, bf16[512,3584]{1,0:T(8,128)(2,1)}, u32[]{:S(2)}) copy-start(bf16[512,3584]{1,0:T(8,128)(2,1)} %get-tuple-element.15.mine_ref) | copy-start | bytes 11010052
  165.9 28.7 %collective-permute-start.2 = (bf16[128,2048]{1,0:T(8,128)(2,1)S(1)}, bf16[128,2048]{1,0:T(8,128)(2,1)S(1)}, u32[]{:S(2)}, u32[]{:S(2)}) collective-permute-start(bf16[128,2048]{1,0:T(8,128)(2,1)S(1)} %fusion.1), channel_id=1, source_target_pairs={{0,0},{1,8},{2,16},{3,24},{8,1},{9,9},{10,17},{11,25},{16,2},{17,1... | collective-permute-start | bytes 1572872 | tf_op jit(solution)/shard_map/ppermute | solution.py:535
  168.9 25.7 %copy-start.7 = (bf16[128,3584]{1,0:T(8,128)(2,1)S(1)}, bf16[128,3584]{1,0:T(8,128)(2,1)}, u32[]{:S(2)}) copy-start(bf16[128,3584]{1,0:T(8,128)(2,1)} %get-tuple-element.20) | copy-start | bytes 2752516
where the time goes:
time: 197 us; the launch traced here: 196 us
  Pallas kernels  152 us (77%)
  waiting for transfers between devices  21.9 us (11%)
  local copies, waits for them, and re-layouts  13.8 us (7%)
  starting transfers between devices  4.09 us (2%)
  other arithmetic  3.5 us (2%)
    pallas_call x1, Pallas kernels, line_exchange(): pl.pallas_call(functools.partial(line_kernel, n, width), out_shape=(jax.S...  113 us
    pallas_call x1, Pallas kernels, fetch_tokens(): pl.pallas_call(functools.partial(fetch_kernel, n), grid=(steps,), out_sha...  26.3 us
    pallas_call x1, Pallas kernels, rotated_grad(): pl.pallas_call(functools.partial(grad_kernel, scaling), grid=(width // ti...  13.3 us
    ppermute x1, waiting for transfers between devices, shards(): input_grad = lax.ppermute(summed, ('fsdp', 'tensor'), swap)  12.4 us
    ppermute x2, waiting for transfers between devices, halve(): came = lax.ppermute(sent, 'tensor', [(t, t ^ bit) for t in range(n_tensor)])  9.45 us
    unnamed x20, local copies, waits for them, and re-layouts  6.6 us
  transfers between devices with their start and end apart: 3, of which 3 were waited for; matrix products, arithmetic and copies ran while one was open for 3% of the time, Pallas kernels for 7%

commit v1 on v0

v1 whole, which is shorter than its diff:
```python
import functools

import jax
import jax.numpy as jnp
from jax import lax
from jax.experimental import pallas as pl
from jax.experimental.pallas import tpu as pltpu
from jax.sharding import PartitionSpec as P

HB = 128


def hadamard_table(length):
    indices = jnp.arange(length, dtype=jnp.int32)
    intersection_bits = jnp.bitwise_and(indices[:, None], indices[None, :])
    parity = jnp.zeros((length, length), jnp.int32)
    for bit_pos in range(length.bit_length() - 1):
        parity = parity + jnp.bitwise_and(jnp.right_shift(intersection_bits, bit_pos), 1)
    return (1 - 2 * (parity % 2)).astype(jnp.bfloat16)


def grad_kernel(scaling, turned_ref, mine_ref, other_ref, sign_ref, table_ref, out_ref, rotated):
    half, width = mine_ref.shape
    for part, ref in enumerate((mine_ref, other_ref)):
        for block in range(width // HB):
            cols = slice(block * HB, (block + 1) * HB)
            signed = ref[:, cols] * sign_ref[:, cols]
            rotated[part * half:(part + 1) * half, cols] = jnp.dot(
                signed, table_ref[...], preferred_element_type=jnp.float32
            ).astype(jnp.bfloat16)
    out_ref[...] = scaling * jnp.dot(turned_ref[...], rotated[...], preferred_element_type=jnp.float32)


def rotated_grad(turned, mine, other, sign_bits):
    rows, total = turned.shape
    half, width = mine.shape
    tile = next(t for t in (512, 256, HB) if width % t == 0)
    signs = (2 * sign_bits - 1).astype(jnp.bfloat16)[None, :]
    scaling = float(1.0 / (HB * total) ** 0.5)
    column = lambda c: (0, c)
    fixed = lambda c: (0, 0)
    return pl.pallas_call(
        functools.partial(grad_kernel, scaling),
        grid=(width // tile,),
        out_shape=jax.ShapeDtypeStruct((rows, width), jnp.float32),
        in_specs=[
            pl.BlockSpec((rows, total), fixed),
            pl.BlockSpec((half, tile), column),
            pl.BlockSpec((half, tile), column),
            pl.BlockSpec((1, tile), column),
            pl.BlockSpec((HB, HB), fixed),
        ],
        out_specs=pl.BlockSpec((rows, tile), column),
        scratch_shapes=[pltpu.VMEM((total, tile), jnp.bfloat16)],
        compiler_params=pltpu.CompilerParams(vmem_limit_bytes=48 * 1024 * 1024),
        cost_estimate=pl.CostEstimate(
            flops=2 * rows * total * width, bytes_accessed=4 * rows * width + 2 * total * width, transcendentals=0
        ),
        name="rotated_grad",
    )(turned, mine, other, signs, hadamard_table(HB))


MESH = pl.DeviceIdType.MESH
LAG = 2


def rotation_table(length):
    table = hadamard_table(HB)
    empty = jnp.zeros_like(table)
    count = length // HB
    return jnp.concatenate(
        [jnp.concatenate([table if i == j else empty for j in range(count)], 1) for i in range(count)], 0
    )


def exchange_kernel(
    n, parts, width, quant, span,
    tokens_hbm, codes_hbm, scales_hbm, cot_hbm, sign_ref, table_ref,
    act_hbm, turned_hbm, rotated_hbm, grad_hbm, last_ref,
    columns, across, turned, weight, scales, cot, act, part, from_left, from_right, mine, other,
    stage, product, total, whole, pair_in, pair_sum, over_in, quarter, landing, grad, pair_last, sum_last, over_last,
    load_sem, fetched, own_sem, act_sem, turned_sem, stage_sem, grad_sem,
    out_sent, out_came, mate_sent, mate_came, over_sent, over_came, relay_sent, relay_came,
    swap_sem, sum_sent, left_came, right_came, up_sent, down_sent, came, cross_sent, cross_came,
    pair_sem, flip_sem, line_sent, line_came, deal_sent, deal_came,
):
    me, t, r = lax.axis_index("fsdp"), lax.axis_index("tensor"), lax.axis_index("replica")
    lane, row = t % 2, t // 2
    mate, over, cross_over, twin = t + 1 - 2 * lane, (t + 2) % 4, 3 - t, 1 - r
    high, low = jnp.minimum(me + 1, n - 1), jnp.maximum(me - 1, 0)
    has_low, has_high = me > 0, me < n - 1
    depth = tokens_hbm.shape[1] // n
    rows = tokens_hbm.shape[0] // parts
    piece, eighth, half = depth // 4, depth // 8, depth // 2
    chunks = weight.shape[0]
    items = parts * chunks
    held = n * rows

    def ds(index, size):
        return pl.ds(pl.multiple_of(index * size, size), size)

    def remote(src, dst, sent, arrival, **device):
        return pltpu.make_async_remote_copy(
            src_ref=src, dst_ref=dst, send_sem=sent, recv_sem=arrival, device_id=device, device_id_type=MESH
        )

    def each(act_on):
        for k in range(1, n):
            for s in (me - k, me + k):
                @pl.when(jnp.logical_and(s >= 0, s < n))
                def _():
                    act_on(s)

    def others(index, count, act_on):
        for k in range(count):
            @pl.when(index != k)
            def _():
                act_on(k)

    def spot(p, s, q):
        return columns.at[p, ds(s, rows), ds(q, piece)]

    def send_out(p, f):
        return remote(
            tokens_hbm.at[ds(p, rows), ds(f * 4 + t, piece)], spot(p, me, t),
            out_sent.at[p, f], out_came.at[p, me], fsdp=f,
        )

    def receive_out(p, s):
        return remote(spot(p, s, t), spot(p, s, t), out_sent.at[p, s], out_came.at[p, s], fsdp=s)

    def to_mate(p, s):
        return remote(spot(p, s, t), spot(p, s, t), mate_sent.at[p, s], mate_came.at[p, s], tensor=mate)

    def to_over(p, s):
        return remote(spot(p, s, t), spot(p, s, t), over_sent.at[p, s], over_came.at[p, s], tensor=over)

    def to_relay(p, s):
        return remote(spot(p, s, over), spot(p, s, over), relay_sent.at[p, s], relay_came.at[p, s], tensor=mate)

    def own(p):
        return pltpu.make_async_copy(
            tokens_hbm.at[ds(p, rows), ds(me, depth)], columns.at[p, ds(me, rows), :], own_sem.at[p]
        )

    def forward(p):
        def go(s):
            receive_out(p, s).wait_recv()
            to_mate(p, s).start()
            to_over(p, s).start()
        each(go)

    def relay(p):
        def go(s):
            to_over(p, s).wait_recv()
            to_relay(p, s).start()
        each(go)

    def finish(p):
        own(p).wait()

        def go(s):
            to_mate(p, s).wait_recv()
            to_relay(p, s).wait_recv()
            send_out(p, s).wait_send()
            to_mate(p, s).wait_send()
            to_over(p, s).wait_send()
            to_relay(p, s).wait_send()
        each(go)

    def share(q):
        return across.at[:, :, ds(q, eighth)]

    swap = remote(
        columns.at[:, :, ds(twin * 4 + t, eighth)], share(t), swap_sem.at[0], swap_sem.at[1], replica=twin
    )
    swap_mate = remote(share(t), share(t), swap_sem.at[2], swap_sem.at[3], tensor=mate)
    swap_over = remote(share(t), share(t), swap_sem.at[4], swap_sem.at[5], tensor=over)
    swap_relay = remote(share(over), share(over), swap_sem.at[6], swap_sem.at[7], tensor=mate)

    def fetch(c):
        return pltpu.make_async_copy(codes_hbm.at[:, ds(c, width)], weight.at[c], fetched.at[c])

    def unpack(c):
        fetch(c).wait()

        def block(b, carry):
            at = ds(b, quant)
            weight[c, at, :] = (
                weight[c, at, :].astype(jnp.float32) * scales[pl.ds(b, 1), ds(c, width)]
            ).astype(jnp.bfloat16)
            return carry

        lax.fori_loop(0, depth // quant, block, 0)

    def blk(ref, s, j):
        start = s * rows if isinstance(s, int) else pl.multiple_of(s * rows, rows)
        return ref.at[j, pl.ds(start, rows), :]

    def move(source, target, s, j, sent, arrival, **device):
        return remote(blk(source, s, j), blk(target, s, j), sent.at[s, j], arrival.at[s, j], **device)

    def sum_up(d, j):
        return move(part, from_left, d, j, sum_sent, left_came, fsdp=high)

    def sum_down(d, j):
        return move(part, from_right, d, j, sum_sent, right_came, fsdp=low)

    def go_up(s, j):
        return move(mine, mine, s, j, up_sent, came, fsdp=high)

    def go_down(s, j):
        return move(mine, mine, s, j, down_sent, came, fsdp=low)

    def cross(s, j):
        return move(mine, other, s, j, cross_sent, cross_came, replica=twin)

    def act_out(j):
        at = (ds(j // chunks, rows), ds(j % chunks, width))
        return pltpu.make_async_copy(act.at[at], act_hbm.at[at], act_sem.at[j])

    def within(j):
        return jnp.logical_and(j >= 0, j < items)

    def project(j):
        part[j] = jnp.dot(
            columns[j // chunks], weight[j % chunks], preferred_element_type=jnp.float32
        ).astype(jnp.bfloat16)

    def turned_out():
        return pltpu.make_async_copy(turned, turned_hbm, turned_sem)

    def stage_out(j, which):
        return pltpu.make_async_copy(
            stage.at[j % 2, which],
            rotated_hbm.at[ds(which * parts + j // chunks, held), ds(j % chunks, width)],
            stage_sem.at[j % 2, which],
        )

    loads = (
        pltpu.make_async_copy(scales_hbm, scales, load_sem.at[0]),
        pltpu.make_async_copy(cot_hbm, cot, load_sem.at[1]),
    )
    loads[0].start()
    for c in range(2):
        fetch(c).start()
    for p in range(parts):
        own(p).start()

    barrier = pltpu.get_barrier_semaphore()
    for k in range(1, n):
        pl.semaphore_signal(barrier, inc=1, device_id={"fsdp": (me + k) % n}, device_id_type=MESH)
    for k in range(1, 4):
        pl.semaphore_signal(barrier, inc=1, device_id={"tensor": (t + k) % 4}, device_id_type=MESH)
    pl.semaphore_signal(barrier, inc=1, device_id={"replica": twin}, device_id_type=MESH)
    pl.semaphore_wait(barrier, n + 3)

    for p in range(parts):
        for k in range(1, n):
            send_out(p, (me + k) % n).start()
    for c in range(2, chunks):
        fetch(c).start()
    loads[1].start()
    loads[0].wait()

    unpack(0)
    unpack(1)
    forward(0)
    unpack(2)
    relay(0)
    unpack(3)
    finish(0)
    loads[1].wait()
    project(0)

    def chain(j, first, owners, applies, arrival, send):
        @pl.when(within(j))
        def _():
            @pl.when(jnp.logical_not(first))
            def _():
                for d in owners:
                    @pl.when(applies(d))
                    def _():
                        arrival[1](d, j).wait_recv()
                        blk(part, d, j)[...] = (
                            blk(part, d, j)[...].astype(jnp.float32)
                            + blk(arrival[0], d, j)[...].astype(jnp.float32)
                        ).astype(jnp.bfloat16)
            for d in owners:
                @pl.when(applies(d))
                def _():
                    send(d, j).start()

    def pair(p, y):
        return remote(
            whole.at[p, :, ds(2 * y + 1 - lane, piece)], pair_in.at[p, y],
            pair_sem.at[0, p, y], pair_sem.at[1, p, y], tensor=mate,
        )

    def pair_final(y):
        return remote(
            whole.at[parts - 1, ds(2 * y + 1 - lane, rows), :], pair_last.at[y],
            pair_sem.at[0, parts - 1, y], pair_sem.at[1, parts - 1, y], tensor=mate,
        )

    def flip(p):
        return remote(
            pair_sum.at[p, 1 - row], over_in.at[p], flip_sem.at[0, p], flip_sem.at[1, p], tensor=over
        )

    flip_final = remote(
        sum_last.at[1 - row], over_last, flip_sem.at[0, parts - 1], flip_sem.at[1, parts - 1], tensor=over
    )

    def line_out(p, f):
        return remote(
            quarter.at[p, ds(f, rows), :], landing.at[p, me], line_sent.at[p, f], line_came.at[p, me], fsdp=f
        )

    def line_in(p, s):
        return remote(
            landing.at[p, s], landing.at[p, s], line_sent.at[p, s], line_came.at[p, s], fsdp=s
        )

    def deal_out(p, s):
        return remote(
            landing.at[p, s], grad.at[ds(p, rows), ds(t, piece)], deal_sent.at[p, s], deal_came.at[p, t], tensor=s
        )

    def deal_in(p, q):
        at = grad.at[ds(p, rows), ds(q, piece)]
        return remote(at, at, deal_sent.at[p, q], deal_came.at[p, q], tensor=q)

    def plus(a, b):
        return (a.astype(jnp.float32) + b.astype(jnp.float32)).astype(jnp.bfloat16)

    def reduce_step(p, lag):
        @pl.when(lag == 0)
        def _():
            for y in range(2):
                pair(p, y).start()

        @pl.when(lag == 1)
        def _():
            for y in range(2):
                pair(p, y).wait()
                pair_sum[p, y] = plus(whole[p, :, ds(2 * y + lane, piece)], pair_in[p, y])
            flip(p).start()

        @pl.when(lag == 3)
        def _():
            flip(p).wait()
            quarter[p] = plus(pair_sum[p, row], over_in[p])
            landing[p, me] = quarter[p, ds(me, rows), :]
            others(me, n, lambda f: line_out(p, f).start())

        @pl.when(lag == 5)
        def _():
            def settle(s):
                line_in(p, s).wait_recv()
                line_out(p, s).wait_send()
            others(me, n, settle)
            grad[ds(p, rows), ds(t, piece)] = landing[p, t]
            others(t, 4, lambda s: deal_out(p, s).start())

        @pl.when(lag == span - 1)
        def _():
            def settle(s):
                deal_in(p, s).wait_recv()
                deal_out(p, s).wait_send()
            others(t, 4, settle)

    reach = LAG * (n - 1)

    def step(i, carry):
        up, down = i - LAG * me, i - LAG * (n - 1 - me)
        chain(up, me == 0, range(n - 1, 0, -1), lambda d: me < d, (from_left, sum_up), sum_up)
        chain(down, me == n - 1, range(n - 1), lambda d: me > d, (from_right, sum_down), sum_down)
        j = i - reach

        @pl.when(within(j))
        def _():
            total[...] = blk(part, me, j)[...].astype(jnp.float32)

            @pl.when(has_low)
            def _():
                sum_up(me, j).wait_recv()
                total[...] += blk(from_left, me, j)[...].astype(jnp.float32)

            @pl.when(has_high)
            def _():
                sum_down(me, j).wait_recv()
                total[...] += blk(from_right, me, j)[...].astype(jnp.float32)

            hidden = total[...]
            sig = jax.nn.sigmoid(hidden)
            at = (ds(j // chunks, rows), ds(j % chunks, width))
            act[at] = (hidden * sig).astype(jnp.bfloat16)
            blk(mine, me, j)[...] = (
                cot[at].astype(jnp.float32) * sig * (1.0 + hidden * (1.0 - sig))
            ).astype(jnp.bfloat16)

            @pl.when(has_high)
            def _():
                go_up(me, j).start()

            @pl.when(has_low)
            def _():
                go_down(me, j).start()

            cross(me, j).start()
            act_out(j).start()

        for k in range(1, n):
            late = i - reach - LAG * k

            @pl.when(jnp.logical_and(within(late), me - k >= 0))
            def _():
                s = me - k
                go_up(s, late).wait_recv()

                @pl.when(has_high)
                def _():
                    go_up(s, late).start()

                cross(s, late).start()

            @pl.when(jnp.logical_and(within(late), me + k < n))
            def _():
                s = me + k
                go_down(s, late).wait_recv()

                @pl.when(has_low)
                def _():
                    go_down(s, late).start()

                cross(s, late).start()

        @pl.when(jnp.logical_and(i >= 2, jnp.logical_and(i <= 2 * (parts - 1), i % 2 == 0)))
        def _():
            finish(i // 2)

        @pl.when(jnp.logical_and(i < 2 * (parts - 1), i % 2 == 0))
        def _():
            forward(1 + i // 2)

        @pl.when(jnp.logical_and(i < 2 * (parts - 1), i % 2 == 1))
        def _():
            relay(1 + i // 2)

        @pl.when(i + 4 < chunks)
        def _():
            unpack(i + 4)

        @pl.when(i + 1 < items)
        def _():
            project(i + 1)

        done = i - 2 * reach

        @pl.when(within(done))
        def _():
            c = done % chunks
            grown = lax.dot_general(
                mine[done], weight[c], (((1,), (1,)), ((), ())), preferred_element_type=jnp.float32
            )

            @pl.when(c == 0)
            def _():
                product[...] = grown

            @pl.when(c > 0)
            def _():
                product[...] += grown

            @pl.when(c == chunks - 1)
            def _():
                whole[done // chunks] = product[...].astype(jnp.bfloat16)

        age = done - (chunks - 1)

        @pl.when(jnp.logical_and(age >= 0, age // chunks < parts - 1))
        def _():
            reduce_step(age // chunks, age % chunks)

        @pl.when(i == items - 1 + 2 * reach)
        def _():
            for y in range(2):
                pair_final(y).start()

        @pl.when(i == 2 * parts)
        def _():
            swap.start()

        @pl.when(i == 2 * parts + 4)
        def _():
            swap.wait()
            swap_mate.start()
            swap_over.start()

        @pl.when(i == 2 * parts + 7)
        def _():
            swap_over.wait()
            swap_relay.start()

        @pl.when(i == 2 * parts + 10)
        def _():
            swap_mate.wait()
            swap_relay.wait()

        flat = i - (2 * parts + 11)

        @pl.when(jnp.logical_and(flat >= 0, flat < parts))
        def _():
            turned[:, ds(flat, held)] = columns[flat, :, ds(r, half)].T

        @pl.when(jnp.logical_and(flat >= parts, flat < 2 * parts))
        def _():
            turned[:, ds(flat, held)] = across[flat - parts].T

        @pl.when(flat == 2 * parts)
        def _():
            turned_out().start()

        late = i - 2 * reach - LAG

        @pl.when(within(late))
        def _():
            @pl.when(late >= 2)
            def _():
                for which in range(2):
                    stage_out(late - 2, which).wait()
            for s in range(n):
                cross(s, late).wait_recv()
            side = table_ref.shape[0]
            for which, ref in enumerate((mine, other)):
                for b in range(width // side):
                    signed = ref[late, :, b * side:(b + 1) * side] * sign_ref[
                        :, pl.ds(pl.multiple_of((late % chunks) * width + b * side, side), side)
                    ]
                    stage[late % 2, which, :, b * side:(b + 1) * side] = jnp.dot(
                        signed, table_ref[...], preferred_element_type=jnp.float32
                    ).astype(jnp.bfloat16)
            for which in range(2):
                stage_out(late, which).start()
            act_out(late).wait()
            for d in range(n):
                @pl.when(me != d)
                def _():
                    sum_up(d, late).wait_send()

                @pl.when(jnp.logical_and(has_high, me >= d))
                def _():
                    go_up(d, late).wait_send()

                @pl.when(jnp.logical_and(has_low, me <= d))
                def _():
                    go_down(d, late).wait_send()

                cross(d, late).wait_send()

        return carry

    lax.fori_loop(0, items + 2 * reach + LAG, step, 0)

    keep = grad.at[pl.ds(0, (parts - 1) * rows), :]
    grad_out = pltpu.make_async_copy(keep, grad_hbm, grad_sem)
    grad_out.start()
    for y in range(2):
        pair_final(y).wait()
        sum_last[y] = plus(whole[parts - 1, ds(2 * y + lane, rows), :], pair_last[y])
    flip_final.start()
    for j in (items - 2, items - 1):
        for which in range(2):
            stage_out(j, which).wait()
    turned_out().wait()
    grad_out.wait()
    flip_final.wait()
    last_ref[...] = plus(sum_last[row], over_last[...])


def exchange(tokens, codes, scales, cotangent, sign_bits, n, parts, width):
    local, cols = cotangent.shape
    depth = codes.shape[0]
    rows, chunks = local // parts, cols // width
    items, held, piece = parts * chunks, n * rows, depth // 4
    bf16, f32 = jnp.bfloat16, jnp.float32
    hbm = pl.BlockSpec(memory_space=pltpu.MemorySpace.HBM)
    vmem = pl.BlockSpec(memory_space=pltpu.VMEM)
    block = pltpu.VMEM((items, held, width), bf16)
    dma = pltpu.SemaphoreType.DMA
    side = 256 if width % 256 == 0 else HB
    return pl.pallas_call(
        functools.partial(exchange_kernel, n, parts, width, depth // scales.shape[0], chunks),
        out_shape=(
            jax.ShapeDtypeStruct(cotangent.shape, bf16),
            jax.ShapeDtypeStruct((depth // 2, 2 * n * local), bf16),
            jax.ShapeDtypeStruct((2 * n * local, cols), bf16),
            jax.ShapeDtypeStruct(((parts - 1) * rows, depth), bf16),
            jax.ShapeDtypeStruct((rows, depth), bf16),
        ),
        in_specs=[hbm] * 4 + [vmem] * 2,
        out_specs=(hbm,) * 4 + (vmem,),
        scratch_shapes=[
            pltpu.VMEM((parts, held, depth), bf16),
            pltpu.VMEM((parts, held, depth // 2), bf16),
            pltpu.VMEM((depth // 2, 2 * n * local), bf16),
            pltpu.VMEM((chunks, depth, width), bf16),
            pltpu.VMEM(scales.shape, f32),
            pltpu.VMEM(cotangent.shape, bf16),
            pltpu.VMEM(cotangent.shape, bf16),
        ]
        + [block] * 5
        + [
            pltpu.VMEM((2, 2, held, width), bf16),
            pltpu.VMEM((held, depth), f32),
            pltpu.VMEM((rows, width), f32),
            pltpu.VMEM((parts, held, depth), bf16),
            pltpu.VMEM((parts - 1, 2, held, piece), bf16),
            pltpu.VMEM((parts - 1, 2, held, piece), bf16),
            pltpu.VMEM((parts - 1, held, piece), bf16),
            pltpu.VMEM((parts - 1, held, piece), bf16),
            pltpu.VMEM((parts - 1, n, rows, piece), bf16),
            pltpu.VMEM((local, depth), bf16),
            pltpu.VMEM((2, rows, depth), bf16),
            pltpu.VMEM((2, rows, depth), bf16),
            pltpu.VMEM((rows, depth), bf16),
            dma((2,)),
            dma((chunks,)),
            dma((parts,)),
            dma((items,)),
            dma,
            dma((2, 2)),
            dma,
        ]
        + [dma((parts, n))] * 8
        + [dma((8,))]
        + [dma((n, items))] * 8
        + [dma((2, parts, 2)), dma((2, parts))]
        + [dma((parts - 1, n))] * 2
        + [dma((parts - 1, 4))] * 2,
        compiler_params=pltpu.CompilerParams(
            collective_id=0, has_side_effects=True, vmem_limit_bytes=63 * 1024 * 1024
        ),
        name="exchange",
    )(
        tokens, codes, scales, cotangent,
        (2 * sign_bits - 1).astype(bf16)[None, :], rotation_table(side),
    )


def product_kernel(scaling, turned_ref, rotated_ref, act_ref, out_ref, act_out_ref):
    out_ref[...] = scaling * jnp.dot(turned_ref[...], rotated_ref[...], preferred_element_type=jnp.float32)
    act_out_ref[...] = act_ref[...]


def weight_product(turned, rotated, activation):
    rows, total = turned.shape
    width, local = rotated.shape[1], activation.shape[0]
    tile = next(t for t in (512, 256, HB) if width % t == 0)
    column = lambda c: (0, c)
    return pl.pallas_call(
        functools.partial(product_kernel, float(1.0 / (HB * total) ** 0.5)),
        grid=(width // tile,),
        out_shape=(
            jax.ShapeDtypeStruct((rows, width), jnp.float32),
            jax.ShapeDtypeStruct(activation.shape, activation.dtype),
        ),
        in_specs=[
            pl.BlockSpec((rows, total), lambda c: (0, 0)),
            pl.BlockSpec((total, tile), column),
            pl.BlockSpec((local, tile), column),
        ],
        out_specs=(pl.BlockSpec((rows, tile), column), pl.BlockSpec((local, tile), column)),
        compiler_params=pltpu.CompilerParams(vmem_limit_bytes=48 * 1024 * 1024),
        cost_estimate=pl.CostEstimate(
            flops=2 * rows * total * width, bytes_accessed=4 * rows * width + 2 * total * width, transcendentals=0
        ),
        name="weight_product",
    )(turned, rotated, activation)


def fits(tokens, codes, scales, cotangent, n_fsdp, n_tensor, parts, width):
    local, cols = cotangent.shape
    depth = codes.shape[0]
    if n_fsdp != 4 or n_tensor != 4 or lax.axis_size("replica") != 2:
        return False
    if local % (16 * parts) or cols % width or cols // width < 7 or depth % 1024 or (n_fsdp * local // parts) % HB:
        return False
    gathered = n_fsdp * local
    room = 2 * depth * cols + 10 * gathered * cols + 15 * gathered * depth + 4 * local * cols
    return room <= 56 * 1024 * 1024


def halve(array, keep, n_tensor, bit):
    lead = lax.dynamic_index_in_dim(array, keep, 0, keepdims=False)
    sent = lax.dynamic_index_in_dim(array, 1 - keep, 0, keepdims=False)
    came = lax.ppermute(sent, "tensor", [(t, t ^ bit) for t in range(n_tensor)])
    return (lead.astype(jnp.float32) + came.astype(jnp.float32)).astype(jnp.bfloat16)


def tensor_reduce(product, n_tensor):
    if n_tensor != 4:
        return lax.psum_scatter(product, "tensor", scatter_dimension=0, tiled=True)
    rows, cols = product.shape
    place = lax.axis_index("tensor")
    chunks = product.reshape(2, 2, rows // 4, cols).swapaxes(0, 1)
    chunks = halve(chunks, place % 2, n_tensor, 1)
    return halve(chunks, place // 2, n_tensor, 2)


def partner(array):
    return lax.ppermute(array, "replica", [(0, 1), (1, 0)])


def shards(tokens, weight_codes, scales, cotangent, sign_bits):
    n_fsdp, n_tensor = lax.axis_size("fsdp"), lax.axis_size("tensor")
    local_tokens = tokens.shape[0]
    shard_rows, hidden_cols = weight_codes.shape
    block_rows = shard_rows // scales.shape[0]
    swap = [(f * n_tensor + t, t * n_tensor + f) for f in range(n_fsdp) for t in range(n_tensor)]
    parts, width = 4, 512
    if fits(tokens, weight_codes, scales, cotangent, n_fsdp, n_tensor, parts, width):
        activation, turned, rotated, early, last = exchange(
            tokens, weight_codes, scales, cotangent, sign_bits, n_fsdp, parts, width
        )
        last = lax.ppermute(last, ("fsdp", "tensor"), swap)
        grad_codes, activation = weight_product(turned, rotated, activation)
        return (activation, jnp.concatenate([early, last], axis=0), grad_codes)
    weight = (
        (
            weight_codes.astype(jnp.float32).reshape(scales.shape[0], block_rows, hidden_cols)
            * scales[:, None, :]
        )
        .reshape(shard_rows, hidden_cols)
        .astype(jnp.bfloat16)
    )
    piece = shard_rows // n_tensor
    own = lax.dynamic_slice_in_dim(
        tokens.reshape(local_tokens, n_fsdp, shard_rows), lax.axis_index("tensor") * piece, piece, 2
    ).reshape(local_tokens, n_fsdp * piece)
    quarter = lax.all_to_all(own, "fsdp", split_axis=1, concat_axis=0, tiled=True)
    columns = lax.all_gather(quarter, "tensor", axis=1, tiled=True)
    half_rows = shard_rows // 2
    replica = lax.axis_index("replica")
    kept = lax.dynamic_slice_in_dim(columns, replica * half_rows, half_rows, 1)
    across = partner(lax.dynamic_slice_in_dim(columns, (1 - replica) * half_rows, half_rows, 1))
    hidden = lax.psum_scatter(
        jnp.dot(columns, weight, preferred_element_type=jnp.float32).astype(jnp.bfloat16),
        "fsdp",
        scatter_dimension=0,
        tiled=True,
    ).astype(jnp.float32)
    sigmoid_val = jax.nn.sigmoid(hidden)
    activation = (hidden * sigmoid_val).astype(jnp.bfloat16)
    hidden_grad = (
        cotangent.astype(jnp.float32) * sigmoid_val * (1.0 + hidden * (1.0 - sigmoid_val))
    ).astype(jnp.bfloat16)
    arrived = lax.all_gather(hidden_grad, "fsdp", axis=0, tiled=True)
    other = partner(arrived)
    product = lax.dot_general(
        arrived, weight, (((1,), (1,)), ((), ())), preferred_element_type=jnp.float32
    ).astype(jnp.bfloat16)
    turned = jnp.concatenate([kept, across], axis=0).T
    if n_fsdp == n_tensor:
        input_grad = lax.ppermute(tensor_reduce(product, n_tensor), ("fsdp", "tensor"), swap)
    else:
        returned = lax.all_to_all(product, "fsdp", split_axis=0, concat_axis=1, tiled=True)
        input_grad = lax.psum_scatter(returned, "tensor", scatter_dimension=1, tiled=True)
    grad_codes = rotated_grad(turned, arrived, other, sign_bits)
    return (activation, input_grad, grad_codes)


def solution(mesh):
    return jax.shard_map(
        shards,
        mesh=mesh,
        in_specs=(
            P(("fsdp", "replica"), None),
            P("fsdp", "tensor"),
            P("fsdp", "tensor"),
            P(("fsdp", "replica"), "tensor"),
            P("tensor"),
        ),
        out_specs=(
            P(("fsdp", "replica"), "tensor"),
            P(("fsdp", "replica"), "tensor"),
            P(("fsdp", "replica"), "tensor"),
        ),
        check_vma=False,
    )
```

time: 197 us -> 166 us (0.84)
  waiting for transfers between devices: 21.9 us -> 0.01 us
  local copies, waits for them, and re-layouts: 13.8 us -> 3.38 us
  Pallas kernels: 152 us -> 154 us
    ppermute x3 -> x1, waiting for transfers between devices: 21.9 us -> 0.01 us  [shards(): last = lax.ppermute(last, ('fsdp', 'tensor'), swap)]
    pallas_call x2 -> x0, local copies, waits for them, and re-layouts: 4.93 us -> none  [the longest x1 2.5 us: fetch_tokens(): pl.pallas_call(functools.partial(fetch_kernel, n), grid=(steps,), out_sha...]
    unnamed x20 -> x6, local copies, waits for them, and re-layouts: 6.6 us -> 2.77 us
    convert_element_type x3 -> x1, other arithmetic: 3.1 us -> 0.73 us  [exchange(): (2 * sign_bits - 1).astype(bf16)[None, :]]
    squeeze x2 -> x0, local copies, waits for them, and re-layouts: 2.14 us -> none  [halve(): sent = lax.dynamic_index_in_dim(array, 1 - keep, 0, keepdims=False)]
    pallas_call x3 -> x2, Pallas kernels: 152 us -> 154 us  [the longest x1 140 us: exchange(): pl.pallas_call(functools.partial(exchange_kernel, n, parts, width, depth...]
    ppermute x3 -> x1, starting transfers between devices: 4.09 us -> 3.33 us  [shards(): last = lax.ppermute(last, ('fsdp', 'tensor'), swap)]
  transfers between devices with their start and end apart: 3 -> 1, of which waited for: 3 -> 0; matrix products, arithmetic and copies ran while one was open for 3% -> 0% of each run, Pallas kernels for 7% -> 8%
where the time goes in v1:
time: 166 us; the launch traced here: 164 us
  Pallas kernels  154 us (93%)
  local copies, waits for them, and re-layouts  3.38 us (2%)
  starting transfers between devices  3.33 us (2%)
  other arithmetic  2.33 us (1%)
    pallas_call x1, Pallas kernels, exchange(): pl.pallas_call(functools.partial(exchange_kernel, n, parts, width, depth...  140 us
    pallas_call x1, Pallas kernels, weight_product(): pl.pallas_call(functools.partial(product_kernel, float(1.0 / (HB * total)...  13.6 us
    ppermute x1, starting transfers between devices, shards(): last = lax.ppermute(last, ('fsdp', 'tensor'), swap)  3.33 us
  transfers between devices with their start and end apart: 1, of which 0 were waited for; matrix products, arithmetic and copies ran while one was open for 0% of the time, Pallas kernels for 8%

profile of v1, /device:TPU:4, one launch (start us, length us, event | category | flops | bytes accessed | tf_op | source)
XLA Modules:
  0.0 163.7 jit_solution(11021653355809411925)
XLA Ops:
  0.6 0.1 fusion.6
  0.7 0.7 add_convert_fusion
  1.4 0.6 broadcast_in_dim.2.sign_ref
  2.1 0.7 fusion.2.table_ref
  2.7 140.3 %exchange.1 = (bf16[128,3584]{1,0:T(8,128)(2,1)}, bf16[1024,1024]{1,0:T(8,128)(2,1)}, bf16[1024,3584]{1,0:T(8,128)(2,1)}, bf16[96,2048]{1,0:T(8,128)(2,1)}, bf16[32,2048]{1,0:T(8,128)(2,1)}) custom-call(bf16[128,8192]{1,0:T(8,128)(2,1)} %tokens_hbm.1, bf16[2048,3584]{1,0:T(8,128)(2,1)} %codes_hbm.1, f32[16,3584]{1,0:T(8,128)} %scales_hbm.1, ...), custom_call_target="tpu_custom_call" | custom-call | tf_op jit(solution)/shard_map/exchange/pallas_call | solution.py:593
  143.1 3.3 %collective-permute-start = (bf16[32,2048]{1,0:T(8,128)(2,1)}, bf16[32,2048]{1,0:T(8,128)(2,1)S(1)}, u32[]{:S(2)}, u32[]{:S(2)}) collective-permute-start(bf16[32,2048]{1,0:T(8,128)(2,1)} %get-tuple-element.15), channel_id=1, source_target_pairs={{0,0},{1,8},{2,16},{3,24},{8,1},{9,9},{10,17},{11,25},{16,2},{17,1... | collective-permute-start | bytes 393224 | tf_op jit(solution)/shard_map/ppermute | solution.py:727
  146.4 0.0 copy-start
  146.4 1.6 copy-done
  148.0 0.0 copy-start.1
  148.0 1.2 copy-done.1
  149.2 0.0 copy-start.2
  149.2 13.6 %weight_product.1 = (f32[1024,3584]{1,0:T(8,128)}, bf16[128,3584]{1,0:T(8,128)(2,1)}) custom-call(bf16[1024,1024]{1,0:T(8,128)(2,1)S(1)} %copy-done, bf16[1024,3584]{1,0:T(8,128)(2,1)} %get-tuple-element.11.rotated_ref, bf16[128,3584]{1,0:T(8,128)(2,1)S(1)} %copy-done.1), custom_call_target="tpu_custom_call" | custom-call | flops 7516192768 | bytes 22020096 | tf_op jit(solution)/shard_map/weight_product/pallas_call | solution.py:662
  162.8 0.0 collective-permute-done
  162.8 0.0 copy-done.2
  162.8 0.8 pad_maximum_fusion
Async XLA Ops:
  143.1 19.7 %collective-permute-start = (bf16[32,2048]{1,0:T(8,128)(2,1)}, bf16[32,2048]{1,0:T(8,128)(2,1)S(1)}, u32[]{:S(2)}, u32[]{:S(2)}) collective-permute-start(bf16[32,2048]{1,0:T(8,128)(2,1)} %get-tuple-element.15), channel_id=1, source_target_pairs={{0,0},{1,8},{2,16},{3,24},{8,1},{9,9},{10,17},{11,25},{16,2},{17,1... | collective-permute-start | bytes 393224 | tf_op jit(solution)/shard_map/ppermute | solution.py:727
  146.4 1.6 copy-start
  148.0 1.2 copy-start.1
  149.2 13.6 %copy-start.2 = (bf16[96,2048]{1,0:T(8,128)(2,1)S(1)}, bf16[96,2048]{1,0:T(8,128)(2,1)}, u32[]{:S(2)}) copy-start(bf16[96,2048]{1,0:T(8,128)(2,1)} %get-tuple-element.14) | copy-start | bytes 1179652

commit v2 on v1

--- a/solution.py
+++ b/solution.py
@@ -64,25 +64,16 @@
 LAG = 2
 
 
-def rotation_table(length):
-    table = hadamard_table(HB)
-    empty = jnp.zeros_like(table)
-    count = length // HB
-    return jnp.concatenate(
-        [jnp.concatenate([table if i == j else empty for j in range(count)], 1) for i in range(count)], 0
-    )
-
-
 def exchange_kernel(
     n, parts, width, quant, span,
-    tokens_hbm, codes_hbm, scales_hbm, cot_hbm, sign_ref, table_ref,
+    tokens_hbm, codes_hbm, scales_hbm, cot_hbm, bits_ref,
     act_hbm, turned_hbm, rotated_hbm, grad_hbm, last_ref,
     columns, across, turned, weight, scales, cot, act, part, from_left, from_right, mine, other,
-    stage, product, total, whole, pair_in, pair_sum, over_in, quarter, landing, grad, pair_last, sum_last, over_last,
+    stage, product, total, table, signs, whole, pair_in, pair_sum, over_in, quarter, landing, grad, pair_last, sum_last, over_last,
     load_sem, fetched, own_sem, act_sem, turned_sem, stage_sem, grad_sem,
-    out_sent, out_came, mate_sent, mate_came, over_sent, over_came, relay_sent, relay_came,
-    swap_sem, sum_sent, left_came, right_came, up_sent, down_sent, came, cross_sent, cross_came,
-    pair_sem, flip_sem, line_sent, line_came, deal_sent, deal_came,
+    out_came, over_came, token_sent, mate_came,
+    swap_sem, came, sent, left_came, right_came, cross_came,
+    pair_sem, flip_sem, line_sem, deal_sem,
 ):
     me, t, r = lax.axis_index("fsdp"), lax.axis_index("tensor"), lax.axis_index("replica")
     lane, row = t % 2, t // 2
@@ -123,20 +114,20 @@
     def send_out(p, f):
         return remote(
             tokens_hbm.at[ds(p, rows), ds(f * 4 + t, piece)], spot(p, me, t),
-            out_sent.at[p, f], out_came.at[p, me], fsdp=f,
+            token_sent.at[p], out_came.at[p, me], fsdp=f,
         )
 
     def receive_out(p, s):
-        return remote(spot(p, s, t), spot(p, s, t), out_sent.at[p, s], out_came.at[p, s], fsdp=s)
+        return remote(spot(p, s, t), spot(p, s, t), token_sent.at[p], out_came.at[p, s], fsdp=s)
 
     def to_mate(p, s):
-        return remote(spot(p, s, t), spot(p, s, t), mate_sent.at[p, s], mate_came.at[p, s], tensor=mate)
+        return remote(spot(p, s, t), spot(p, s, t), token_sent.at[p], mate_came.at[p], tensor=mate)
 
     def to_over(p, s):
-        return remote(spot(p, s, t), spot(p, s, t), over_sent.at[p, s], over_came.at[p, s], tensor=over)
+        return remote(spot(p, s, t), spot(p, s, t), token_sent.at[p], over_came.at[p, s], tensor=over)
 
     def to_relay(p, s):
-        return remote(spot(p, s, over), spot(p, s, over), relay_sent.at[p, s], relay_came.at[p, s], tensor=mate)
+        return remote(spot(p, s, over), spot(p, s, over), token_sent.at[p], mate_came.at[p], tensor=mate)
 
     def own(p):
         return pltpu.make_async_copy(
@@ -158,15 +149,10 @@
 
     def finish(p):
         own(p).wait()
-
-        def go(s):
-            to_mate(p, s).wait_recv()
-            to_relay(p, s).wait_recv()
-            send_out(p, s).wait_send()
-            to_mate(p, s).wait_send()
-            to_over(p, s).wait_send()
-            to_relay(p, s).wait_send()
-        each(go)
+        lead = columns.at[p, pl.ds(0, (n - 1) * rows), :]
+        two = columns.at[p, pl.ds(0, (n - 1) * rows), pl.ds(0, 2 * piece)]
+        remote(two, two, token_sent.at[p], mate_came.at[p], tensor=mate).wait_recv()
+        remote(lead, lead, token_sent.at[p], mate_came.at[p], tensor=mate).wait_send()
 
     def share(q):
         return across.at[:, :, ds(q, eighth)]
@@ -197,27 +183,32 @@
         start = s * rows if isinstance(s, int) else pl.multiple_of(s * rows, rows)
         return ref.at[j, pl.ds(start, rows), :]
 
-    def move(source, target, s, j, sent, arrival, **device):
-        return remote(blk(source, s, j), blk(target, s, j), sent.at[s, j], arrival.at[s, j], **device)
-
-    def sum_up(d, j):
-        return move(part, from_left, d, j, sum_sent, left_came, fsdp=high)
-
-    def sum_down(d, j):
-        return move(part, from_right, d, j, sum_sent, right_came, fsdp=low)
+    def span_of(ref, j, start, count):
+        return ref.at[j, pl.ds(start * rows, count * rows), :]
+
+    def sum_up(m, j):
+        at = (j, m + 1, n - 1 - m)
+        return remote(span_of(part, *at), span_of(from_left, *at), sent.at[j], left_came.at[j], fsdp=high)
+
+    def sum_down(m, j):
+        at = (j, 0, m)
+        return remote(span_of(part, *at), span_of(from_right, *at), sent.at[j], right_came.at[j], fsdp=low)
+
+    def move(target, s, j, arrival, **device):
+        return remote(blk(mine, s, j), blk(target, s, j), sent.at[j], arrival, **device)
 
     def go_up(s, j):
-        return move(mine, mine, s, j, up_sent, came, fsdp=high)
+        return move(mine, s, j, came.at[s, j], fsdp=high)
 
     def go_down(s, j):
-        return move(mine, mine, s, j, down_sent, came, fsdp=low)
+        return move(mine, s, j, came.at[s, j], fsdp=low)
 
     def cross(s, j):
-        return move(mine, other, s, j, cross_sent, cross_came, replica=twin)
-
-    def act_out(j):
-        at = (ds(j // chunks, rows), ds(j % chunks, width))
-        return pltpu.make_async_copy(act.at[at], act_hbm.at[at], act_sem.at[j])
+        return move(other, s, j, cross_came.at[j], replica=twin)
+
+    def act_out(p):
+        at = act.at[ds(p, rows), :]
+        return pltpu.make_async_copy(at, act_hbm.at[ds(p, rows), :], act_sem.at[p])
 
     def within(j):
         return jnp.logical_and(j >= 0, j < items)
@@ -261,6 +252,16 @@
     for c in range(2, chunks):
         fetch(c).start()
     loads[1].start()
+    side = table.shape[0]
+    first_index = lax.broadcasted_iota(jnp.int32, (side, side), 0)
+    second_index = lax.broadcasted_iota(jnp.int32, (side, side), 1)
+    parity = jnp.bitwise_and(jnp.bitwise_and(first_index, second_index), HB - 1)
+    for shift in (4, 2, 1):
+        parity = jnp.bitwise_xor(parity, jnp.right_shift(parity, shift))
+    entry = (1 - 2 * jnp.bitwise_and(parity, 1)).astype(jnp.float32)
+    table[...] = jnp.where(jnp.bitwise_xor(first_index, second_index) < HB, entry, 0.0).astype(jnp.bfloat16)
+    for b in range(bits_ref.shape[0]):
+        signs[:, b * HB:(b + 1) * HB] = (2 * bits_ref[b:b + 1, :] - 1).astype(jnp.float32)
     loads[0].wait()
 
     unpack(0)
@@ -273,34 +274,37 @@
     loads[1].wait()
     project(0)
 
-    def chain(j, first, owners, applies, arrival, send):
-        @pl.when(within(j))
-        def _():
-            @pl.when(jnp.logical_not(first))
-            def _():
-                for d in owners:
-                    @pl.when(applies(d))
-                    def _():
-                        arrival[1](d, j).wait_recv()
-                        blk(part, d, j)[...] = (
-                            blk(part, d, j)[...].astype(jnp.float32)
-                            + blk(arrival[0], d, j)[...].astype(jnp.float32)
-                        ).astype(jnp.bfloat16)
-            for d in owners:
-                @pl.when(applies(d))
-                def _():
-                    send(d, j).start()
+    def plus(a, b):
+        return (a.astype(jnp.float32) + b.astype(jnp.float32)).astype(jnp.bfloat16)
+
+    def chain_up(m, j):
+        if m > 0:
+            sum_up(m - 1, j).wait_recv()
+        if m < n - 1:
+            if m > 0:
+                at = pl.ds((m + 1) * rows, (n - 1 - m) * rows)
+                part[j, at, :] = plus(part[j, at, :], from_left[j, at, :])
+            sum_up(m, j).start()
+
+    def chain_down(m, j):
+        if m < n - 1:
+            sum_down(m + 1, j).wait_recv()
+        if m > 0:
+            if m < n - 1:
+                at = pl.ds(0, m * rows)
+                part[j, at, :] = plus(part[j, at, :], from_right[j, at, :])
+            sum_down(m, j).start()
 
     def pair(p, y):
         return remote(
             whole.at[p, :, ds(2 * y + 1 - lane, piece)], pair_in.at[p, y],
-            pair_sem.at[0, p, y], pair_sem.at[1, p, y], tensor=mate,
+            pair_sem.at[0, p], pair_sem.at[1, p], tensor=mate,
         )
 
     def pair_final(y):
         return remote(
             whole.at[parts - 1, ds(2 * y + 1 - lane, rows), :], pair_last.at[y],
-            pair_sem.at[0, parts - 1, y], pair_sem.at[1, parts - 1, y], tensor=mate,
+            pair_sem.at[0, parts - 1], pair_sem.at[1, parts - 1], tensor=mate,
         )
 
     def flip(p):
@@ -314,25 +318,21 @@
 
     def line_out(p, f):
         return remote(
-            quarter.at[p, ds(f, rows), :], landing.at[p, me], line_sent.at[p, f], line_came.at[p, me], fsdp=f
-        )
-
-    def line_in(p, s):
-        return remote(
-            landing.at[p, s], landing.at[p, s], line_sent.at[p, s], line_came.at[p, s], fsdp=s
-        )
+            quarter.at[p, ds(f, rows), :], landing.at[p, me], line_sem.at[0, p], line_sem.at[1, p], fsdp=f
+        )
+
+    def line_all(p):
+        at = landing.at[p, pl.ds(0, n - 1)]
+        return remote(at, at, line_sem.at[0, p], line_sem.at[1, p], fsdp=high)
 
     def deal_out(p, s):
         return remote(
-            landing.at[p, s], grad.at[ds(p, rows), ds(t, piece)], deal_sent.at[p, s], deal_came.at[p, t], tensor=s
-        )
-
-    def deal_in(p, q):
-        at = grad.at[ds(p, rows), ds(q, piece)]
-        return remote(at, at, deal_sent.at[p, q], deal_came.at[p, q], tensor=q)
-
-    def plus(a, b):
-        return (a.astype(jnp.float32) + b.astype(jnp.float32)).astype(jnp.bfloat16)
+            landing.at[p, s], grad.at[ds(p, rows), ds(t, piece)], deal_sem.at[0, p], deal_sem.at[1, p], tensor=s
+        )
+
+    def deal_all(p):
+        at = landing.at[p, pl.ds(0, 3)]
+        return remote(at, at, deal_sem.at[0, p], deal_sem.at[1, p], tensor=mate)
 
     def reduce_step(p, lag):
         @pl.when(lag == 0)
@@ -342,8 +342,8 @@
 
         @pl.when(lag == 1)
         def _():
+            remote(pair_in.at[p], pair_in.at[p], pair_sem.at[0, p], pair_sem.at[1, p], tensor=mate).wait()
             for y in range(2):
-                pair(p, y).wait()
                 pair_sum[p, y] = plus(whole[p, :, ds(2 * y + lane, piece)], pair_in[p, y])
             flip(p).start()
 
@@ -356,26 +356,28 @@
 
         @pl.when(lag == 5)
         def _():
-            def settle(s):
-                line_in(p, s).wait_recv()
-                line_out(p, s).wait_send()
-            others(me, n, settle)
+            line_all(p).wait()
             grad[ds(p, rows), ds(t, piece)] = landing[p, t]
             others(t, 4, lambda s: deal_out(p, s).start())
 
         @pl.when(lag == span - 1)
         def _():
-            def settle(s):
-                deal_in(p, s).wait_recv()
-                deal_out(p, s).wait_send()
-            others(t, 4, settle)
+            deal_all(p).wait()
 
     reach = LAG * (n - 1)
 
     def step(i, carry):
-        up, down = i - LAG * me, i - LAG * (n - 1 - me)
-        chain(up, me == 0, range(n - 1, 0, -1), lambda d: me < d, (from_left, sum_up), sum_up)
-        chain(down, me == n - 1, range(n - 1), lambda d: me > d, (from_right, sum_down), sum_down)
+        for m in range(n):
+            up, down = i - LAG * m, i - LAG * (n - 1 - m)
+
+            @pl.when(jnp.logical_and(me == m, within(up)))
+            def _():
+                chain_up(m, up)
+
+            @pl.when(jnp.logical_and(me == m, within(down)))
+            def _():
+                chain_down(m, down)
+
         j = i - reach
 
         @pl.when(within(j))
@@ -384,12 +386,10 @@
 
             @pl.when(has_low)
             def _():
-                sum_up(me, j).wait_recv()
                 total[...] += blk(from_left, me, j)[...].astype(jnp.float32)
 
             @pl.when(has_high)
             def _():
-                sum_down(me, j).wait_recv()
                 total[...] += blk(from_right, me, j)[...].astype(jnp.float32)
 
             hidden = total[...]
@@ -409,7 +409,10 @@
                 go_down(me, j).start()
 
             cross(me, j).start()
-            act_out(j).start()
+
+            @pl.when(j % chunks == chunks - 1)
+            def _():
+                act_out(j // chunks).start()
 
         for k in range(1, n):
             late = i - reach - LAG * k
@@ -530,34 +533,32 @@
             def _():
                 for which in range(2):
                     stage_out(late - 2, which).wait()
-            for s in range(n):
-                cross(s, late).wait_recv()
-            side = table_ref.shape[0]
+            remote(mine.at[late], other.at[late], sent.at[late], cross_came.at[late], replica=twin).wait_recv()
             for which, ref in enumerate((mine, other)):
                 for b in range(width // side):
-                    signed = ref[late, :, b * side:(b + 1) * side] * sign_ref[
-                        :, pl.ds(pl.multiple_of((late % chunks) * width + b * side, side), side)
-                    ]
+                    signed = (
+                        ref[late, :, b * side:(b + 1) * side].astype(jnp.float32)
+                        * signs[:, pl.ds(pl.multiple_of((late % chunks) * width + b * side, side), side)]
+                    ).astype(jnp.bfloat16)
                     stage[late % 2, which, :, b * side:(b + 1) * side] = jnp.dot(
-                        signed, table_ref[...], preferred_element_type=jnp.float32
+                        signed, table[...], preferred_element_type=jnp.float32
                     ).astype(jnp.bfloat16)
             for which in range(2):
                 stage_out(late, which).start()
-            act_out(late).wait()
-            for d in range(n):
-                @pl.when(me != d)
-                def _():
-                    sum_up(d, late).wait_send()
-
-                @pl.when(jnp.logical_and(has_high, me >= d))
-                def _():
-                    go_up(d, late).wait_send()
-
-                @pl.when(jnp.logical_and(has_low, me <= d))
-                def _():
-                    go_down(d, late).wait_send()
-
-                cross(d, late).wait_send()
+
+            def sent_all(count):
+                at = mine.at[pl.ds(0, count)]
+                remote(at, at, sent.at[late], cross_came.at[late], replica=twin).wait_send()
+
+            at_end = jnp.logical_or(me == 0, me == n - 1)
+
+            @pl.when(at_end)
+            def _():
+                sent_all(2)
+
+            @pl.when(jnp.logical_not(at_end))
+            def _():
+                sent_all(3)
 
         return carry
 
@@ -566,8 +567,10 @@
     keep = grad.at[pl.ds(0, (parts - 1) * rows), :]
     grad_out = pltpu.make_async_copy(keep, grad_hbm, grad_sem)
     grad_out.start()
+    remote(
+        pair_last, pair_last, pair_sem.at[0, parts - 1], pair_sem.at[1, parts - 1], tensor=mate
+    ).wait()
     for y in range(2):
-        pair_final(y).wait()
         sum_last[y] = plus(whole[parts - 1, ds(2 * y + lane, rows), :], pair_last[y])
     flip_final.start()
     for j in (items - 2, items - 1):
@@ -575,6 +578,8 @@
             stage_out(j, which).wait()
     turned_out().wait()
     grad_out.wait()
+    for p in range(parts):
+        act_out(p).wait()
     flip_final.wait()
     last_ref[...] = plus(sum_last[row], over_last[...])
 
@@ -599,7 +604,7 @@
             jax.ShapeDtypeStruct(((parts - 1) * rows, depth), bf16),
             jax.ShapeDtypeStruct((rows, depth), bf16),
         ),
-        in_specs=[hbm] * 4 + [vmem] * 2,
+        in_specs=[hbm] * 4 + [vmem],
         out_specs=(hbm,) * 4 + (vmem,),
         scratch_shapes=[
             pltpu.VMEM((parts, held, depth), bf16),
@@ -615,6 +620,8 @@
             pltpu.VMEM((2, 2, held, width), bf16),
             pltpu.VMEM((held, depth), f32),
             pltpu.VMEM((rows, width), f32),
+            pltpu.VMEM((side, side), bf16),
+            pltpu.VMEM((1, cols), f32),
             pltpu.VMEM((parts, held, depth), bf16),
             pltpu.VMEM((parts - 1, 2, held, piece), bf16),
             pltpu.VMEM((parts - 1, 2, held, piece), bf16),
@@ -628,25 +635,23 @@
             dma((2,)),
             dma((chunks,)),
             dma((parts,)),
-            dma((items,)),
+            dma((parts,)),
             dma,
             dma((2, 2)),
             dma,
         ]
-        + [dma((parts, n))] * 8
+        + [dma((parts, n))] * 2
+        + [dma((parts,))] * 2
         + [dma((8,))]
-        + [dma((n, items))] * 8
-        + [dma((2, parts, 2)), dma((2, parts))]
-        + [dma((parts - 1, n))] * 2
-        + [dma((parts - 1, 4))] * 2,
+        + [dma((n, items))]
+        + [dma((items,))] * 4
+        + [dma((2, parts))] * 2
+        + [dma((2, parts - 1))] * 2,
         compiler_params=pltpu.CompilerParams(
             collective_id=0, has_side_effects=True, vmem_limit_bytes=63 * 1024 * 1024
         ),
         name="exchange",
-    )(
-        tokens, codes, scales, cotangent,
-        (2 * sign_bits - 1).astype(bf16)[None, :], rotation_table(side),
-    )
+    )(tokens, codes, scales, cotangent, sign_bits.reshape(cols // HB, HB))
 
 
 def product_kernel(scaling, turned_ref, rotated_ref, act_ref, out_ref, act_out_ref):
@@ -672,7 +677,7 @@
             pl.BlockSpec((local, tile), column),
         ],
         out_specs=(pl.BlockSpec((rows, tile), column), pl.BlockSpec((local, tile), column)),
-        compiler_params=pltpu.CompilerParams(vmem_limit_bytes=48 * 1024 * 1024),
+        compiler_params=pltpu.CompilerParams(vmem_limit_bytes=63 * 1024 * 1024),
         cost_estimate=pl.CostEstimate(
             flops=2 * rows * total * width, bytes_accessed=4 * rows * width + 2 * total * width, transcendentals=0
         ),

time: 166 us -> 154 us (0.928)
  Pallas kernels: 154 us -> 148 us
  local copies, waits for them, and re-layouts: 3.38 us -> 0.01 us
    pallas_call x1, Pallas kernels: 140 us -> 133 us  [exchange(): pl.pallas_call(functools.partial(exchange_kernel, n, parts, width, depth...]
    unnamed x6 -> x2, local copies, waits for them, and re-layouts: 2.77 us -> 0.01 us
  transfers between devices with their start and end apart: 1 -> 1, of which waited for: 0 -> 0; matrix products, arithmetic and copies ran while one was open for 0% -> 0% of each run, Pallas kernels for 8% -> 10%
where the time goes in v2:
time: 154 us; the launch traced here: 152 us
  Pallas kernels  148 us (96%)
  starting transfers between devices  2.51 us (2%)
    pallas_call x1, Pallas kernels, exchange(): pl.pallas_call(functools.partial(exchange_kernel, n, parts, width, depth...  133 us
    pallas_call x1, Pallas kernels, weight_product(): pl.pallas_call(functools.partial(product_kernel, float(1.0 / (HB * total)...  14.4 us
  transfers between devices with their start and end apart: 1, of which 0 were waited for; matrix products, arithmetic and copies ran while one was open for 0% of the time, Pallas kernels for 10%

profile of v2, /device:TPU:4, one launch (start us, length us, event | category | flops | bytes accessed | tf_op | source)
XLA Modules:
  0.0 151.6 jit_solution(8592105075953336890)
XLA Ops:
  0.6 133.1 %exchange.1 = (bf16[128,3584]{1,0:T(8,128)(2,1)}, bf16[1024,1024]{1,0:T(8,128)(2,1)}, bf16[1024,3584]{1,0:T(8,128)(2,1)}, bf16[96,2048]{1,0:T(8,128)(2,1)}, bf16[32,2048]{1,0:T(8,128)(2,1)}) custom-call(bf16[128,8192]{1,0:T(8,128)(2,1)} %tokens_hbm.1, bf16[2048,3584]{1,0:T(8,128)(2,1)} %codes_hbm.1, f32[16,3584]{1,0:T(8,128)} %scales_hbm.1, ...), custom_call_target="tpu_custom_call" | custom-call | tf_op jit(solution)/shard_map/exchange/pallas_call | solution.py:598
  133.8 2.5 %collective-permute-start = (bf16[32,2048]{1,0:T(8,128)(2,1)}, bf16[32,2048]{1,0:T(8,128)(2,1)S(1)}, u32[]{:S(2)}, u32[]{:S(2)}) collective-permute-start(bf16[32,2048]{1,0:T(8,128)(2,1)} %get-tuple-element.15), channel_id=1, source_target_pairs={{0,0},{1,8},{2,16},{3,24},{8,1},{9,9},{10,17},{11,25},{16,2},{17,1... | collective-permute-start | bytes 393224 | tf_op jit(solution)/shard_map/ppermute | solution.py:732
  136.3 0.0 copy-start
  136.3 14.4 %weight_product.1 = (f32[1024,3584]{1,0:T(8,128)}, bf16[128,3584]{1,0:T(8,128)(2,1)}) custom-call(bf16[1024,1024]{1,0:T(8,128)(2,1)} %get-tuple-element.10.turned_ref, bf16[1024,3584]{1,0:T(8,128)(2,1)} %get-tuple-element.11.rotated_ref, bf16[128,3584]{1,0:T(8,128)(2,1)} %get-tuple-element.12.act_ref), custom_call_target="tpu_custom_call" | custom-call | flops 7516192768 | bytes 22020096 | tf_op jit(solution)/shard_map/weight_product/pallas_call | solution.py:667
  150.7 0.0 collective-permute-done
  150.7 0.0 copy-done
  150.7 0.8 pad_maximum_fusion
Async XLA Ops:
  133.8 16.9 %collective-permute-start = (bf16[32,2048]{1,0:T(8,128)(2,1)}, bf16[32,2048]{1,0:T(8,128)(2,1)S(1)}, u32[]{:S(2)}, u32[]{:S(2)}) collective-permute-start(bf16[32,2048]{1,0:T(8,128)(2,1)} %get-tuple-element.15), channel_id=1, source_target_pairs={{0,0},{1,8},{2,16},{3,24},{8,1},{9,9},{10,17},{11,25},{16,2},{17,1... | collective-permute-start | bytes 393224 | tf_op jit(solution)/shard_map/ppermute | solution.py:732
  136.3 14.4 %copy-start = (bf16[96,2048]{1,0:T(8,128)(2,1)S(1)}, bf16[96,2048]{1,0:T(8,128)(2,1)}, u32[]{:S(2)}) copy-start(bf16[96,2048]{1,0:T(8,128)(2,1)} %get-tuple-element.14) | copy-start | bytes 1179652

commit v3 on v2

--- a/solution.py
+++ b/solution.py
@@ -352,17 +352,6 @@
             flip(p).wait()
             quarter[p] = plus(pair_sum[p, row], over_in[p])
             landing[p, me] = quarter[p, ds(me, rows), :]
-            others(me, n, lambda f: line_out(p, f).start())
-
-        @pl.when(lag == 5)
-        def _():
-            line_all(p).wait()
-            grad[ds(p, rows), ds(t, piece)] = landing[p, t]
-            others(t, 4, lambda s: deal_out(p, s).start())
-
-        @pl.when(lag == span - 1)
-        def _():
-            deal_all(p).wait()
 
     reach = LAG * (n - 1)
 
@@ -486,10 +475,36 @@
         def _():
             reduce_step(age // chunks, age % chunks)
 
+        for p in range(parts - 1):
+            begin = items + LAG * n // 2 - 1 + 2 * p
+
+            @pl.when(i == begin)
+            def _():
+                others(me, n, lambda f: line_out(p, f).start())
+
+            @pl.when(i == begin + 3)
+            def _():
+                line_all(p).wait()
+                grad[ds(p, rows), ds(t, piece)] = landing[p, t]
+                others(t, 4, lambda s: deal_out(p, s).start())
+
+            @pl.when(i == begin + 5)
+            def _():
+                deal_all(p).wait()
+
         @pl.when(i == items - 1 + 2 * reach)
         def _():
             for y in range(2):
                 pair_final(y).start()
+
+        @pl.when(i == items + 2 * reach)
+        def _():
+            remote(
+                pair_last, pair_last, pair_sem.at[0, parts - 1], pair_sem.at[1, parts - 1], tensor=mate
+            ).wait()
+            for y in range(2):
+                sum_last[y] = plus(whole[parts - 1, ds(2 * y + lane, rows), :], pair_last[y])
+            flip_final.start()
 
         @pl.when(i == 2 * parts)
         def _():
@@ -567,12 +582,6 @@
     keep = grad.at[pl.ds(0, (parts - 1) * rows), :]
     grad_out = pltpu.make_async_copy(keep, grad_hbm, grad_sem)
     grad_out.start()
-    remote(
-        pair_last, pair_last, pair_sem.at[0, parts - 1], pair_sem.at[1, parts - 1], tensor=mate
-    ).wait()
-    for y in range(2):
-        sum_last[y] = plus(whole[parts - 1, ds(2 * y + lane, rows), :], pair_last[y])
-    flip_final.start()
     for j in (items - 2, items - 1):
         for which in range(2):
             stage_out(j, which).wait()

time: 154 us -> 153 us (level)
  Pallas kernels: 148 us -> 146 us
    pallas_call x1, Pallas kernels: 133 us -> 131 us  [exchange(): pl.pallas_call(functools.partial(exchange_kernel, n, parts, width, depth...]
where the time goes in v3:
time: 153 us; the launch traced here: 150 us
  Pallas kernels  146 us (95%)
  starting transfers between devices  2.96 us (2%)
    pallas_call x1, Pallas kernels, exchange(): pl.pallas_call(functools.partial(exchange_kernel, n, parts, width, depth...  131 us
    pallas_call x1, Pallas kernels, weight_product(): pl.pallas_call(functools.partial(product_kernel, float(1.0 / (HB * total)...  14.4 us
  transfers between devices with their start and end apart: 1, of which 0 were waited for; matrix products, arithmetic and copies ran while one was open for 0% of the time, Pallas kernels for 10%

profile of v3, /device:TPU:4, one launch (start us, length us, event | category | flops | bytes accessed | tf_op | source)
XLA Modules:
  0.0 150.0 jit_solution(13998309054008770975)
XLA Ops:
  0.6 131.1 %exchange.1 = (bf16[128,3584]{1,0:T(8,128)(2,1)}, bf16[1024,1024]{1,0:T(8,128)(2,1)}, bf16[1024,3584]{1,0:T(8,128)(2,1)}, bf16[96,2048]{1,0:T(8,128)(2,1)}, bf16[32,2048]{1,0:T(8,128)(2,1)}) custom-call(bf16[128,8192]{1,0:T(8,128)(2,1)} %tokens_hbm.1, bf16[2048,3584]{1,0:T(8,128)(2,1)} %codes_hbm.1, f32[16,3584]{1,0:T(8,128)} %scales_hbm.1, ...), custom_call_target="tpu_custom_call" | custom-call | tf_op jit(solution)/shard_map/exchange/pallas_call | solution.py:607
  131.7 3.0 %collective-permute-start = (bf16[32,2048]{1,0:T(8,128)(2,1)}, bf16[32,2048]{1,0:T(8,128)(2,1)S(1)}, u32[]{:S(2)}, u32[]{:S(2)}) collective-permute-start(bf16[32,2048]{1,0:T(8,128)(2,1)} %get-tuple-element.15), channel_id=1, source_target_pairs={{0,0},{1,8},{2,16},{3,24},{8,1},{9,9},{10,17},{11,25},{16,2},{17,1... | collective-permute-start | bytes 393224 | tf_op jit(solution)/shard_map/ppermute | solution.py:741
  134.7 0.0 copy-start
  134.7 14.4 %weight_product.1 = (f32[1024,3584]{1,0:T(8,128)}, bf16[128,3584]{1,0:T(8,128)(2,1)}) custom-call(bf16[1024,1024]{1,0:T(8,128)(2,1)} %get-tuple-element.10.turned_ref, bf16[1024,3584]{1,0:T(8,128)(2,1)} %get-tuple-element.11.rotated_ref, bf16[128,3584]{1,0:T(8,128)(2,1)} %get-tuple-element.12.act_ref), custom_call_target="tpu_custom_call" | custom-call | flops 7516192768 | bytes 22020096 | tf_op jit(solution)/shard_map/weight_product/pallas_call | solution.py:676
  149.1 0.0 collective-permute-done
  149.1 0.0 copy-done
  149.1 0.8 pad_maximum_fusion
Async XLA Ops:
  131.7 17.4 %collective-permute-start = (bf16[32,2048]{1,0:T(8,128)(2,1)}, bf16[32,2048]{1,0:T(8,128)(2,1)S(1)}, u32[]{:S(2)}, u32[]{:S(2)}) collective-permute-start(bf16[32,2048]{1,0:T(8,128)(2,1)} %get-tuple-element.15), channel_id=1, source_target_pairs={{0,0},{1,8},{2,16},{3,24},{8,1},{9,9},{10,17},{11,25},{16,2},{17,1... | collective-permute-start | bytes 393224 | tf_op jit(solution)/shard_map/ppermute | solution.py:741
  134.7 14.4 %copy-start = (bf16[96,2048]{1,0:T(8,128)(2,1)S(1)}, bf16[96,2048]{1,0:T(8,128)(2,1)}, u32[]{:S(2)}) copy-start(bf16[96,2048]{1,0:T(8,128)(2,1)} %get-tuple-element.14) | copy-start | bytes 1179652
